TPU v7x, 256 devices: a whole 4x4x8 slice. The times are simulated.
256 devices in a mesh: grp: 8 (over z), ep: 32 (over y, x, core).
Axes of the slice: x: 4, y: 4, z: 8, core: 2. Of those that a mesh axis runs over, the one named last changes fastest.
Arguments:
- pol_hidden: bfloat16 [10240, 1024], P(('grp', 'ep')), may hold values from -80 to 80
- ref_hidden: bfloat16 [10240, 1024], P(('grp', 'ep')), may hold values from -80 to 80
- pol_routes: int32 [10240, 8], P(('grp', 'ep')), may hold values from 0 to 63, all different within a row; in each aligned block of 40 rows (0 to 39, 40 to 79, ...) at most 7 rows name the same one
- ref_routes: int32 [10240, 8], P(('grp', 'ep')), may hold values from 0 to 63, all different within a row; in each aligned block of 40 rows (0 to 39, 40 to 79, ...) at most 7 rows name the same one
- pol_gates: float32 [10240, 8], P(('grp', 'ep')), may hold values from 0.02 to 0.3
- ref_gates: float32 [10240, 8], P(('grp', 'ep')), may hold values from 0.02 to 0.3
- w_gate: bfloat16 [64, 1024, 384], P('ep'), may hold values from -0.1875 to 0.1875
- w_up: bfloat16 [64, 1024, 384], P('ep'), may hold values from -0.1875 to 0.1875
- w_down: bfloat16 [64, 384, 1024], P('ep'), may hold values from -0.3125 to 0.3125
- norm_gain: float32 [1024], replicated, may hold values from 0.5 to 1.5
- vocab_head: bfloat16 [77824, 1024], P(('grp', 'ep')), may hold values from -2 to 2
- targets: int32 [10240], P(('grp', 'ep')), may hold values from 0 to 77823
- seq_lengths: int32 [256], replicated, may hold values from 1 to 1024, 10240 in all
- owners: int32 [256], replicated, may hold values from 0 to 255, each once
Outputs:
- token_ratio: float32 [10240], P(('grp', 'ep'))
- owned_mean: float32 [256], P(('grp', 'ep'))
Inputs may be any that keep to these rules, and one draw needn't show every extreme that they name: `pol_routes`: each row names 8 different experts; among the 40 rows of one device no expert is named by more than 7 rows, a bound that some block reaches. `ref_routes`: each row names 8 different experts; among the 40 rows of one device no expert is named by more than 7 rows, a bound that some block reaches. `seq_lengths`: the lengths sum to 10240; the longest is exactly 1024. `owners`: every device index appears exactly once.
All inputs are finite; a program needn't handle non-finite values.
Results may differ from a plain program's by a relative error of at most 0.0062.
Values may be sent and summed in bfloat16 or wider, within the bound.
A program may use at most 128 MiB of HBM per device.

v0:
```python
import jax
import jax.numpy as jnp
from jax import lax
from jax.sharding import PartitionSpec as P


def joined_2(value, axis, join):
    pieces = jax.tree.map(lambda part: lax.all_gather(part, axis), value)
    head = jax.tree.map(lambda part: part[0], pieces)
    tail = jax.tree.map(lambda part: part[1:], pieces)
    so_far, _ = lax.scan(lambda so_far, share: (join(so_far, share), None), head, tail)
    return so_far


def combine_stats(earlier_part, second):
    peak = jnp.maximum(earlier_part[0], second[0])
    totals = earlier_part[1] * jnp.exp(earlier_part[0] - peak) + second[1] * jnp.exp(
        second[0] - peak
    )
    return (peak, totals, earlier_part[2] + second[2])


def vocab_stats(row_block, weights, vocab_ids, wanted):
    logits = jnp.einsum("td,vd->tv", row_block, weights, preferred_element_type=jnp.float32)
    peak = jnp.max(logits, axis=1)
    totals = jnp.sum(jnp.exp(logits - peak[:, None]), axis=1)
    picked = jnp.sum(jnp.where(vocab_ids[None, :] == wanted[:, None], logits, 0.0), axis=1)
    return (peak, totals, picked)


def expert_tables(routes, gates, experts, capacity):
    route_hits = routes[:, :, None] == jnp.arange(experts, dtype=jnp.int32)[None, None, :]
    members = jnp.sum(route_hits.astype(jnp.int32), axis=1)
    earlier = jnp.cumsum(members, axis=0) - members
    placed = (members[:, :, None] > 0) & (
        earlier[:, :, None] == jnp.arange(capacity, dtype=jnp.int32)[None, None, :]
    )
    weight = jnp.sum(jnp.where(route_hits, gates[:, :, None], 0.0), axis=1)
    tok_count = routes.shape[0]
    picker = placed.astype(jnp.bfloat16).reshape(tok_count, experts * capacity)
    mixing = (weight[:, :, None] * placed.astype(jnp.float32)).reshape(
        tok_count, experts * capacity
    )
    return (picker, mixing)


def local(
    pol_hidden,
    ref_hidden,
    pol_routes,
    ref_routes,
    pol_gates,
    ref_gates,
    w_gate,
    w_up,
    w_down,
    norm_gain,
    vocab_head,
    targets,
    seq_lengths,
    owners,
):
    groups = lax.axis_size("ep")
    device_index = lax.axis_index(("grp", "ep"))
    local_experts = w_gate.shape[0]
    experts = local_experts * groups
    tok_count = pol_hidden.shape[0]
    width = pol_hidden.shape[1]
    fanout = pol_routes.shape[1]
    capacity = tok_count * fanout // experts + 2
    pol_pick, pol_mixing = expert_tables(pol_routes, pol_gates, experts, capacity)
    ref_pick, ref_mixing = expert_tables(ref_routes, ref_gates, experts, capacity)
    pol_send = jnp.einsum(
        "ts,td->sd", pol_pick, pol_hidden, preferred_element_type=jnp.float32
    ).astype(jnp.bfloat16)
    ref_send = jnp.einsum(
        "ts,td->sd", ref_pick, ref_hidden, preferred_element_type=jnp.float32
    ).astype(jnp.bfloat16)
    pol_send = pol_send.reshape(groups, local_experts, capacity, width)
    ref_send = ref_send.reshape(groups, local_experts, capacity, width)
    pol_part = lax.all_to_all(pol_send, "ep", split_axis=0, concat_axis=0, tiled=True)
    ref_part = lax.all_to_all(ref_send, "ep", split_axis=0, concat_axis=0, tiled=True)
    slots = pol_part.shape[2]
    joined = jnp.concatenate((pol_part, ref_part), axis=2)
    gate_act = jnp.einsum("nesd,edf->nesf", joined, w_gate, preferred_element_type=jnp.float32)
    up_act = jnp.einsum("nesd,edf->nesf", joined, w_up, preferred_element_type=jnp.float32)
    inner = (jax.nn.silu(gate_act) * up_act).astype(jnp.bfloat16)
    outputs = jnp.einsum(
        "nesf,efd->nesd", inner, w_down, preferred_element_type=jnp.float32
    ).astype(jnp.bfloat16)
    pol_back = lax.all_to_all(outputs[:, :, :slots], "ep", split_axis=0, concat_axis=0, tiled=True)
    ref_back = lax.all_to_all(outputs[:, :, slots:], "ep", split_axis=0, concat_axis=0, tiled=True)

    def mix_back(hidden, mixing, back):
        rows_back = back.reshape(experts * capacity, width).astype(jnp.float32)
        mixed = hidden.astype(jnp.float32) + jnp.dot(
            mixing, rows_back, precision=lax.Precision.HIGHEST
        )
        scale = lax.rsqrt(jnp.mean(mixed * mixed, axis=1, keepdims=True) + 1e-06)
        return (mixed * scale * norm_gain).astype(jnp.bfloat16)

    pol_normed = mix_back(pol_hidden, pol_mixing, pol_back)
    ref_normed = mix_back(ref_hidden, ref_mixing, ref_back)
    vocab_rows = vocab_head.shape[0]
    band = lax.axis_index("grp")
    pol_col, ref_col, wanted = (
        lax.all_gather(pol_normed, "grp", axis=0, tiled=True),
        lax.all_gather(ref_normed, "grp", axis=0, tiled=True),
        lax.all_gather(targets, "grp", axis=0, tiled=True),
    )
    col_count = wanted.shape[0]
    floor_value = jnp.full((2, col_count), -1e30, jnp.float32)
    blank = jnp.zeros((2, col_count), jnp.float32)
    piece = lax.all_gather(vocab_head, "ep", axis=0, tiled=True)
    count = piece.shape[0]
    place = jnp.arange(count, dtype=jnp.int32)
    vocab_ids = band * groups * vocab_rows + place
    pol_stats = vocab_stats(pol_col, piece, vocab_ids, wanted)
    ref_stats = vocab_stats(ref_col, piece, vocab_ids, wanted)
    fresh = tuple(
        (jnp.stack((pol_part, ref_part)) for pol_part, ref_part in zip(pol_stats, ref_stats))
    )
    stats = combine_stats((floor_value, blank, blank), fresh)
    peak, totals, picked = joined_2(stats, "grp", combine_stats)
    logprob = picked - (peak + jnp.log(totals))
    mine = lax.dynamic_slice_in_dim(logprob, band * tok_count, tok_count, axis=1)
    token_ratio = mine[0] - mine[1]
    offsets = jnp.cumsum(seq_lengths) - seq_lengths
    positions = device_index * tok_count + jnp.arange(tok_count, dtype=jnp.int32)
    inside = (positions[:, None] >= offsets[None, :]) & (
        positions[:, None] < (offsets + seq_lengths)[None, :]
    )
    partial_value = jnp.dot(
        token_ratio, inside.astype(jnp.float32), precision=lax.Precision.HIGHEST
    ) / seq_lengths.astype(jnp.float32)
    sums = lax.psum(partial_value, ("grp", "ep"))
    owned = jnp.sum(jnp.where(owners == device_index, sums, 0.0)).reshape(1)
    return (token_ratio, owned)


def solution(mesh):
    return jax.shard_map(
        local,
        mesh=mesh,
        in_specs=(
            P(("grp", "ep"), None),
            P(("grp", "ep"), None),
            P(("grp", "ep"), None),
            P(("grp", "ep"), None),
            P(("grp", "ep"), None),
            P(("grp", "ep"), None),
            P("ep", None, None),
            P("ep", None, None),
            P("ep", None, None),
            P(),
            P(("grp", "ep"), None),
            P(("grp", "ep")),
            P(),
            P(),
        ),
        out_specs=(P(("grp", "ep")), P(("grp", "ep"))),
        check_vma=False,
    )
```

profile of v0, /device:TPU:1, one launch (start us, length us, event | category | flops | bytes accessed | tf_op | source)
XLA Modules:
  0.0 389.7 jit_solution(15554492775969641314)
XLA Ops:
  7.2 0.7 all-gather.4.cloned.1.call-update
  7.9 0.8 copy.62
  8.9 0.4 copy-done.13
  9.4 0.6 copy-done.9
  10.4 0.6 copy-done.18
  11.0 0.4 convolution_convert_fusion.1
  11.8 2.0 copy.67
  13.7 8.7 %all-to-all-start = ((bf16[32,2,7,1024]{3,1,2,0:T(2,128)(2,1)}), bf16[32,2,7,1024]{3,1,2,0:T(2,128)(2,1)S(1)}, u32[]{:S(2)}, u32[]{:S(2)}) async-start(bf16[32,2,7,1024]{3,1,2,0:T(2,128)(2,1)} %copy.67), calls=%async_computation | async-start | bytes 1835008 | tf_op jit(solution)/shard_map/all_to_all | solution.py:81
  22.7 0.4 copy-done.15
  23.2 0.6 copy-done.11
  24.1 1.4 convolution_convert_fusion
  25.5 1.4 reshape.318
  27.0 2.0 copy.71
  28.9 12.9 %all-to-all-done = bf16[32,2,7,1024]{3,1,2,0:T(2,128)(2,1)S(1)} async-done(((bf16[32,2,7,1024]{3,1,2,0:T(2,128)(2,1)}), bf16[32,2,7,1024]{3,1,2,0:T(2,128)(2,1)S(1)}, u32[]{:S(2)}, u32[]{:S(2)}) %all-to-all-start) | async-done | bytes 917536 | tf_op jit(solution)/shard_map/all_to_all | solution.py:81
  41.8 0.9 copy-done.2
  42.7 5.4 %all-to-all-start.1 = ((bf16[32,2,7,1024]{3,1,2,0:T(2,128)(2,1)}), bf16[32,2,7,1024]{3,1,2,0:T(2,128)(2,1)}, u32[]{:S(2)}, u32[]{:S(2)}) async-start(bf16[32,2,7,1024]{3,1,2,0:T(2,128)(2,1)} %copy.71), calls=%async_computation.1 | async-start | bytes 1835008 | tf_op jit(solution)/shard_map/all_to_all | solution.py:82
  48.2 1.4 copy_dynamic-update-slice_fusion.1
  49.6 14.5 %all-to-all-done.1 = bf16[32,2,7,1024]{3,1,2,0:T(2,128)(2,1)} async-done(((bf16[32,2,7,1024]{3,1,2,0:T(2,128)(2,1)}), bf16[32,2,7,1024]{3,1,2,0:T(2,128)(2,1)}, u32[]{:S(2)}, u32[]{:S(2)}) %all-to-all-start.1) | async-done | bytes 917536 | tf_op jit(solution)/shard_map/all_to_all | solution.py:82
  64.1 1.5 copy_dynamic-update-slice_fusion
  65.8 2.2 fusion.9
  68.0 5.2 %convert_bitcast_fusion = bf16[32,2,14,1024]{3,0,2,1:T(8,128)(2,1)} fusion(bf16[2,384,1024]{2,1,0:T(8,128)(2,1)S(1)} %copy-done, bf16[32,2,14,1024]{3,0,2,1:T(8,128)(2,1)S(1)} %copy_dynamic-update-slice_fusion, bf16[2,1024,384]{2,1,0:T(8,128)(2,1)} %param.23, f32[32,2,14,384]{3,0,2,1:T(8,128)} %fusion.9), kind=kOutput, calls=%fused_computation.12 | convolution fusion | flops 1412268032 | bytes 8192000 | tf_op jit(solution)/shard_map/nesf,efd->nesd/dot_general | solution.py:88
  73.2 1.9 fusion.44
  75.2 1.9 copy.78
  77.1 3.9 all-to-all-start.3
  81.8 1.9 copy.74
  83.7 21.1 %all-to-all-done.3 = bf16[32,2,7,1024]{3,1,2,0:T(2,128)(2,1)S(1)} async-done(((bf16[32,2,7,1024]{3,1,2,0:T(2,128)(2,1)}), bf16[32,2,7,1024]{3,1,2,0:T(2,128)(2,1)S(1)}, u32[]{:S(2)}, u32[]{:S(2)}) %all-to-all-start.3) | async-done | bytes 917536 | tf_op jit(solution)/shard_map/all_to_all | solution.py:92
  104.8 6.1 %all-to-all-start.2 = ((bf16[32,2,7,1024]{3,1,2,0:T(2,128)(2,1)}), bf16[32,2,7,1024]{3,1,2,0:T(2,128)(2,1)S(1)}, u32[]{:S(2)}, u32[]{:S(2)}) async-start(bf16[32,2,7,1024]{3,1,2,0:T(2,128)(2,1)} %copy.74), calls=%async_computation.2 | async-start | bytes 1835008 | tf_op jit(solution)/shard_map/all_to_all | solution.py:91
  111.0 0.7 mul.94
  112.2 0.6 dynamic-slice
  113.7 20.4 %all-reduce = s32[320]{0:T(512)S(1)} all-reduce(s32[320]{0:T(512)S(1)} %dynamic-update-slice), channel_id=1, replica_groups=mesh['grp'=8,'ep'=32] {'grp'}, use_global_device_ids=true, to_apply=%add | all-reduce | flops 320 | bytes 2560
  134.0 0.6 iota_add_fusion.1
  134.7 0.6 fusion.43
  135.4 0.6 iota_add_fusion
  136.3 1.2 reshape.320
  138.1 0.6 copy-done.3
  138.7 0.7 multiply_reduce_fusion
  139.4 1.7 multiply_reduce_fusion.1
  141.2 20.2 %all_gather.26 = bf16[320,1024]{1,0:T(8,128)(2,1)S(1)} all-gather(bf16[40,1024]{1,0:T(8,128)(2,1)S(1)} %get-tuple-element.71), channel_id=1, replica_groups=mesh['grp'=8,'ep'=32] {'grp'}, dimensions={0}, use_global_device_ids=true | all-gather | bytes 737280 | tf_op jit(solution)/shard_map/all_gather | solution.py:107
  161.4 20.5 %all_gather.28 = bf16[320,1024]{1,0:T(8,128)(2,1)S(1)} all-gather(bf16[40,1024]{1,0:T(8,128)(2,1)S(1)} %get-tuple-element.72), channel_id=1, replica_groups=mesh['grp'=8,'ep'=32] {'grp'}, dimensions={0}, use_global_device_ids=true | all-gather | bytes 737280 | tf_op jit(solution)/shard_map/all_gather | solution.py:108
  181.9 13.4 %fusion.45 = (f32[320]{0:T(512)S(1)}, f32[320,9728]{1,0:T(8,128)}) fusion(bf16[320,1024]{1,0:T(8,128)(2,1)S(1)} %all_gather.26, bf16[9728,1024]{1,0:T(8,128)(2,1)} %all-gather.4.cloned.1.call-done), kind=kOutput, calls=%fused_computation.84 | convolution fusion | flops 6378454528 | bytes 33031424 | tf_op jit(solution)/shard_map/td,vd->tv/dot_general | solution.py:24
  195.3 13.5 %fusion.46 = (f32[320]{0:T(512)S(1)}, f32[320,9728]{1,0:T(8,128)}) fusion(bf16[320,1024]{1,0:T(8,128)(2,1)S(1)} %all_gather.28, bf16[9728,1024]{1,0:T(8,128)(2,1)} %all-gather.4.cloned.1.call-done), kind=kOutput, calls=%fused_computation.85 | convolution fusion | flops 6378454528 | bytes 33031424 | tf_op jit(solution)/shard_map/td,vd->tv/dot_general | solution.py:24
  208.8 11.5 %fusion.2 = (f32[320]{0:T(512)S(1)}, f32[320]{0:T(512)S(1)}, f32[320]{0:T(512)S(1)}, f32[320]{0:T(512)S(1)}) fusion(f32[320,9728]{1,0:T(8,128)} %get-tuple-element.80, s32[9728]{0:T(1024)S(1)} %copy-done.17, s32[320]{0:T(512)S(1)} %all-reduce, f32[320]{0:T(512)S(1)} %get-tuple-element.79, f32[320,9728]{1,0:T(8,128)} %get-tuple-element.82, ...), kind=kLoop, calls=%fused_computation.8 | loop fusion | flops 28015360 | bytes 24951552 | tf_op jit(solution)/shard_map/reduce_sum | solution.py:27
  220.3 18.0 %all-gather.1 = f32[8,2,320]{2,1,0:T(2,128)S(1)} all-gather(f32[1,2,320]{2,1,0:T(2,128)S(1)} %maximum_bitcast_fusion), channel_id=2, replica_groups=mesh['grp'=8,'ep'=32] {'grp'}, dimensions={0}, use_global_device_ids=true | all-gather | bytes 23040 | tf_op jit(solution)/shard_map/all_gather | solution.py:8
  238.4 18.0 %all_gather.30 = f32[8,2,320]{2,1,0:T(2,128)S(1)} all-gather(f32[1,2,320]{2,1,0:T(2,128)S(1)} %get-tuple-element.73), channel_id=1, replica_groups=mesh['grp'=8,'ep'=32] {'grp'}, dimensions={0}, use_global_device_ids=true | all-gather | bytes 23040 | tf_op jit(solution)/shard_map/all_gather | solution.py:8
  256.5 18.0 %all_gather.29 = f32[8,2,320]{2,1,0:T(2,128)S(1)} all-gather(f32[1,2,320]{2,1,0:T(2,128)S(1)} %get-tuple-element.74), channel_id=1, replica_groups=mesh['grp'=8,'ep'=32] {'grp'}, dimensions={0}, use_global_device_ids=true | all-gather | bytes 23040 | tf_op jit(solution)/shard_map/all_gather | solution.py:8
  274.9 0.5 fusion.42
  275.7 106.6 %psum.7 = f32[256]{0:T(256)S(1)} all-reduce(f32[256]{0:T(256)S(1)} %convert_divide_fusion), channel_id=1, replica_groups=mesh['grp'=8,'ep'=32] {'grp','ep'}, use_global_device_ids=true, to_apply=%region_18.19 | all-reduce | flops 256 | bytes 2048 | tf_op jit(solution)/shard_map/psum | solution.py:136
  382.2 0.6 fusion.39
  (125 shorter events, 5.3 us)
Async XLA Ops:
  7.2 60.8 %copy-start = (bf16[2,384,1024]{2,1,0:T(8,128)(2,1)S(1)}, bf16[2,384,1024]{2,1,0:T(8,128)(2,1)}, u32[]{:S(2)}) copy-start(bf16[2,384,1024]{2,1,0:T(8,128)(2,1)} %param.24) | copy-start | bytes 4718596
  7.2 3.8 copy-start.7
  7.2 174.7 %all-gather.4.cloned.1.call-start = ((), (), s32[]{:S(2)}) async-start(), calls=%async_computation.4 | async-start | bytes 20545536 | tf_op jit(solution)/shard_map/all_gather | solution.py:114
  8.7 0.6 copy-start.13
  9.4 0.6 copy-start.9
  10.4 0.6 copy-start.18
  11.7 10.7 %copy-start.22 = (s32[40,8]{0,1:T(8,128)S(1)}, s32[40,8]{0,1:T(8,128)}, u32[]{:S(2)}) copy-start(s32[40,8]{0,1:T(8,128)} %param.19) | copy-start | bytes 3844
  13.7 10.4 %copy-start.5 = (bf16[40,1024]{1,0:T(8,128)(2,1)S(1)}, bf16[40,1024]{1,0:T(8,128)(2,1)}, u32[]{:S(2)}) copy-start(bf16[40,1024]{1,0:T(8,128)(2,1)} %param.17) | copy-start | bytes 245764
  13.7 10.4 %copy-start.19 = (s32[448]{0:T(512)S(1)}, s32[448]{0:T(512)}, u32[]{:S(2)}) copy-start(s32[448]{0:T(512)} %copy-done.18) | copy-start | bytes 5380
  13.7 28.1 %all-to-all-start = ((bf16[32,2,7,1024]{3,1,2,0:T(2,128)(2,1)}), bf16[32,2,7,1024]{3,1,2,0:T(2,128)(2,1)S(1)}, u32[]{:S(2)}, u32[]{:S(2)}) async-start(bf16[32,2,7,1024]{3,1,2,0:T(2,128)(2,1)} %copy.67), calls=%async_computation | async-start | bytes 1835008 | tf_op jit(solution)/shard_map/all_to_all | solution.py:81
  22.5 0.6 copy-start.15
  23.2 0.6 copy-start.11
  41.8 0.9 copy-start.2
  42.7 21.4 %all-to-all-start.1 = ((bf16[32,2,7,1024]{3,1,2,0:T(2,128)(2,1)}), bf16[32,2,7,1024]{3,1,2,0:T(2,128)(2,1)}, u32[]{:S(2)}, u32[]{:S(2)}) async-start(bf16[32,2,7,1024]{3,1,2,0:T(2,128)(2,1)} %copy.71), calls=%async_computation.1 | async-start | bytes 1835008 | tf_op jit(solution)/shard_map/all_to_all | solution.py:82
  64.1 1.7 copy-start.4
  75.2 5.8 %copy-start.23 = (f32[40,8]{0,1:T(8,128)S(1)}, f32[40,8]{0,1:T(8,128)}, u32[]{:S(2)}) copy-start(f32[40,8]{0,1:T(8,128)} %param.21) | copy-start | bytes 3844
  75.2 5.9 %copy-start.16 = (s32[40,8]{1,0:T(8,128)S(1)}, s32[40,8]{1,0:T(8,128)}, u32[]{:S(2)}) copy-start(s32[40,8]{1,0:T(8,128)} %copy-done.15) | copy-start | bytes 3844
  75.2 6.1 %copy-start.12 = (s32[40,64]{0,1:T(8,128)S(1)}, s32[40,64]{0,1:T(8,128)}, u32[]{:S(2)}) copy-start(s32[40,64]{0,1:T(8,128)} %copy-done.11) | copy-start | bytes 30724
  77.1 4.4 %copy-start.24 = (f32[40,8]{0,1:T(8,128)S(1)}, f32[40,8]{0,1:T(8,128)}, u32[]{:S(2)}) copy-start(f32[40,8]{0,1:T(8,128)} %param.20) | copy-start | bytes 3844
  77.1 4.4 %copy-start.14 = (s32[40,8]{1,0:T(8,128)S(1)}, s32[40,8]{1,0:T(8,128)}, u32[]{:S(2)}) copy-start(s32[40,8]{1,0:T(8,128)} %copy-done.13) | copy-start | bytes 3844
  77.1 27.7 %all-to-all-start.3 = ((bf16[32,2,7,1024]{3,1,2,0:T(2,128)(2,1)}), bf16[32,2,7,1024]{3,1,2,0:T(2,128)(2,1)S(1)}, u32[]{:S(2)}, u32[]{:S(2)}) async-start(bf16[32,2,7,1024]{3,1,2,0:T(2,128)(2,1)} %copy.78), calls=%async_computation.3 | async-start | bytes 1835008 | tf_op jit(solution)/shard_map/all_to_all | solution.py:92
  81.8 29.2 %copy-start.10 = (s32[40,64]{0,1:T(8,128)S(1)}, s32[40,64]{0,1:T(8,128)}, u32[]{:S(2)}) copy-start(s32[40,64]{0,1:T(8,128)} %copy-done.9) | copy-start | bytes 30724
  81.8 30.0 %copy-start.20 = (s32[256]{0:T(256)S(1)}, s32[256]{0:T(256)}, u32[]{:S(2)}) copy-start(s32[256]{0:T(256)} %param.28) | copy-start | bytes 3076
  81.8 30.4 %copy-start.28 = (u32[256]{0:T(256)S(1)}, u32[256]{0:T(256)}, u32[]{:S(2)}) copy-start(u32[256]{0:T(256)} %constant.68) | copy-start | bytes 3076
  81.8 31.6 %copy-start.27 = (s32[40]{0:T(128)S(1)}, s32[40]{0:T(128)}, u32[]{:S(2)}) copy-start(s32[40]{0:T(128)} %param.27) | copy-start | bytes 484
  104.8 32.7 %all-to-all-start.2 = ((bf16[32,2,7,1024]{3,1,2,0:T(2,128)(2,1)}), bf16[32,2,7,1024]{3,1,2,0:T(2,128)(2,1)S(1)}, u32[]{:S(2)}, u32[]{:S(2)}) async-start(bf16[32,2,7,1024]{3,1,2,0:T(2,128)(2,1)} %copy.74), calls=%async_computation.2 | async-start | bytes 1835008 | tf_op jit(solution)/shard_map/all_to_all | solution.py:91
  137.5 1.2 copy-start.3
  137.5 1.2 copy-start.6
  137.8 1.6 copy-start.8
  138.7 2.4 copy-start.21
  195.3 13.5 %copy-start.17 = (s32[9728]{0:T(1024)S(1)}, s32[9728]{0:T(1024)}, u32[]{:S(2)}) copy-start(s32[9728]{0:T(1024)} %iota_add_fusion) | copy-start | bytes 116740
  208.8 66.7 %copy-start.26 = (s32[256]{0:T(256)S(1)}, s32[256]{0:T(256)}, u32[]{:S(2)}) copy-start(s32[256]{0:T(256)} %get-tuple-element.67) | copy-start | bytes 3076
  208.8 66.7 %copy-start.29 = (s32[40]{0:T(128)S(1)}, s32[40]{0:T(128)}, u32[]{:S(2)}) copy-start(s32[40]{0:T(128)} %iota_add_fusion.1) | copy-start | bytes 484
  208.8 173.4 %copy-start.25 = (s32[256]{0:T(256)S(1)}, s32[256]{0:T(256)}, u32[]{:S(2)}) copy-start(s32[256]{0:T(256)} %param.29) | copy-start | bytes 3076
  208.8 174.0 %copy-start.1 = (bf16[2,384,1024]{2,1,0:T(8,128)(2,1)S(1)}, bf16[2,384,1024]{2,1,0:T(8,128)(2,1)}, u32[]{:S(2)}) copy-start(bf16[2,384,1024]{2,1,0:T(8,128)(2,1)} %param.24) | copy-start | bytes 4718596
Sparse Core Ops, SparseCore 0:
  10.6 105.0 all-gather.3
where the time goes:
time: 391 us; the launch traced here: 390 us
  blocking collectives  222 us (57%)
  waiting for transfers between devices  49.2 us (13%)
  matrix products  38.7 us (10%)
  local copies, waits for them, and re-layouts  24.4 us (6%)
  starting transfers between devices  24.2 us (6%)
  other arithmetic  16.1 us (4%)
  between operations  15.3 us (4%)
    psum x1, blocking collectives, local(): sums = lax.psum(partial_value, ('grp', 'ep'))  107 us
    all_gather x3, blocking collectives, joined_2(): pieces = jax.tree.map(lambda part: lax.all_gather(part, axis), value)  54 us
    dot_general x2, matrix products, vocab_stats(): jnp.einsum('td,vd->tv', row_block, weights, preferred_element_type=jnp.fl...  26.9 us
    all_to_all x1, waiting for transfers between devices, local(): lax.all_to_all(outputs[:, :, slots:], 'ep', split_axis=0, concat_axis=0,...  21.1 us
    all_gather x1, blocking collectives, local(): lax.all_gather(ref_normed, 'grp', axis=0, tiled=True)  20.5 us
    unnamed x1, blocking collectives  20.4 us
    all_gather x1, blocking collectives, local(): lax.all_gather(pol_normed, 'grp', axis=0, tiled=True)  20.2 us
    all_to_all x1, waiting for transfers between devices, local(): lax.all_to_all(ref_send, 'ep', split_axis=0, concat_axis=0, tiled=True)  14.5 us
  transfers between devices with their start and end apart: 5, of which 3 were waited for; matrix products, arithmetic and copies ran while one was open for 9% of the time, Pallas kernels for 0%

commit v1 on v0

--- a/solution.py
+++ b/solution.py
@@ -1,31 +1,190 @@
 import jax
 import jax.numpy as jnp
 from jax import lax
+from jax.experimental import pallas as pl
+from jax.experimental.pallas import tpu as pltpu
 from jax.sharding import PartitionSpec as P
 
-
-def joined_2(value, axis, join):
-    pieces = jax.tree.map(lambda part: lax.all_gather(part, axis), value)
-    head = jax.tree.map(lambda part: part[0], pieces)
-    tail = jax.tree.map(lambda part: part[1:], pieces)
-    so_far, _ = lax.scan(lambda so_far, share: (join(so_far, share), None), head, tail)
-    return so_far
-
-
-def combine_stats(earlier_part, second):
-    peak = jnp.maximum(earlier_part[0], second[0])
-    totals = earlier_part[1] * jnp.exp(earlier_part[0] - peak) + second[1] * jnp.exp(
-        second[0] - peak
-    )
-    return (peak, totals, earlier_part[2] + second[2])
-
-
-def vocab_stats(row_block, weights, vocab_ids, wanted):
-    logits = jnp.einsum("td,vd->tv", row_block, weights, preferred_element_type=jnp.float32)
-    peak = jnp.max(logits, axis=1)
-    totals = jnp.sum(jnp.exp(logits - peak[:, None]), axis=1)
-    picked = jnp.sum(jnp.where(vocab_ids[None, :] == wanted[:, None], logits, 0.0), axis=1)
-    return (peak, totals, picked)
+MESH = pl.DeviceIdType.MESH
+PLANE = 16
+NT = (((1,), (1,)), ((), ()))
+
+
+def head_kernel(x_ref, d_ref, hz_ref, out_ref, xbuf, dbuf, hbuf, stat, lse,
+                hsem, xsend, xrecv, dsend, drecv, ssend, srecv, csend, crecv):
+    z = lax.axis_index("grp")
+    ep = lax.axis_index("ep")
+    slot = ep // 2
+    core = ep % 2
+    zs = lax.axis_size("grp")
+    rows = x_ref.shape[0]
+    vrows = hz_ref.shape[1]
+    cols = 2 * zs
+
+    def plane_peer(j):
+        return {"ep": ((slot + j) % PLANE) * 2 + core}
+
+    def col_peer(j):
+        other = (z * 2 + core + j) % cols
+        return {"grp": other // 2, "ep": slot * 2 + other % 2}
+
+    barrier = pltpu.get_barrier_semaphore()
+    for j in range(1, PLANE):
+        pl.semaphore_signal(barrier, inc=1, device_id=plane_peer(j), device_id_type=MESH)
+    for j in range(1, cols):
+        pl.semaphore_signal(barrier, inc=1, device_id=col_peer(j), device_id_type=MESH)
+    pl.semaphore_wait(barrier, PLANE - 1 + cols - 1)
+
+    mine = pl.ds(pl.multiple_of(slot * rows, 16), rows)
+    xs, ds_ = [], []
+    for j in range(1, PLANE):
+        cp = pltpu.make_async_remote_copy(
+            src_ref=x_ref, dst_ref=xbuf.at[mine, :], send_sem=xsend.at[j], recv_sem=xrecv.at[j],
+            device_id=plane_peer(j), device_id_type=MESH)
+        cp.start()
+        xs.append(cp)
+        cd = pltpu.make_async_remote_copy(
+            src_ref=d_ref, dst_ref=dbuf.at[mine, :], send_sem=dsend.at[j], recv_sem=drecv.at[j],
+            device_id=plane_peer(j), device_id_type=MESH)
+        cd.start()
+        ds_.append(cd)
+    hown = pltpu.make_async_copy(hz_ref, hbuf.at[core], hsem.at[0])
+    hown.start()
+    hsib = pltpu.make_async_remote_copy(
+        src_ref=hz_ref, dst_ref=hbuf.at[core], send_sem=hsem.at[1], recv_sem=hsem.at[2],
+        device_id={"ep": slot * 2 + (1 - core)}, device_id_type=MESH)
+    hsib.start()
+    xown = pltpu.make_async_copy(x_ref, xbuf.at[mine, :], xsend.at[0])
+    xown.start()
+    down = pltpu.make_async_copy(d_ref, dbuf.at[mine, :], dsend.at[0])
+    down.start()
+    hown.wait()
+    xown.wait()
+    down.wait()
+    hsib.wait()
+    for cp in xs:
+        cp.wait()
+    for cd in ds_:
+        cd.wait()
+
+    stat[slot] = jnp.zeros(stat.shape[1:], jnp.float32)
+    lane = lax.broadcasted_iota(jnp.int32, (8, 128), 1)
+    weights = jnp.where(lane == 0, 1.0, jnp.where(lane == 1, 64.0, jnp.where(lane == 2, 4096.0, 0.0)))
+    weights = weights.astype(jnp.bfloat16)
+    tile = 256
+    place = lax.broadcasted_iota(jnp.int32, (vrows, tile), 0)
+
+    def tile_body(t, carry):
+        rs = pl.ds(pl.multiple_of(t * tile, tile), tile)
+        xt = xbuf[rs, :]
+        wanted = lax.dot_general(weights, dbuf[rs, :], NT, preferred_element_type=jnp.float32)
+        wanted = wanted[0:1, :].astype(jnp.int32)
+
+        def block(b, state):
+            m, s, p = state
+            logits = lax.dot_general(hbuf[b // zs, b % zs], xt, NT, preferred_element_type=jnp.float32)
+            peak = jnp.maximum(m, jnp.max(logits, axis=0, keepdims=True))
+            base = ((b % zs) * (2 * PLANE) + slot * 2 + b // zs) * vrows
+            total = s * jnp.exp(m - peak) + jnp.sum(jnp.exp(logits - peak), axis=0, keepdims=True)
+            hit = place == (wanted - base)
+            got = p + jnp.sum(jnp.where(hit, logits, 0.0), axis=0, keepdims=True)
+            return (peak, total, got)
+
+        zero = jnp.zeros((1, tile), jnp.float32)
+        m, s, p = lax.fori_loop(0, cols, block, (zero - 1e30, zero, zero), unroll=2)
+        for k, v in enumerate((m, s, p)):
+            both = jnp.concatenate([v[:, :128], v[:, 128:]], axis=0)
+            stat[slot, k, pl.ds(t * 2, 2), :] = both
+        return carry
+
+    lax.fori_loop(0, PLANE * rows // tile, tile_body, 0)
+
+    ss = []
+    for j in range(1, PLANE):
+        cp = pltpu.make_async_remote_copy(
+            src_ref=stat.at[slot], dst_ref=stat.at[slot], send_sem=ssend.at[j], recv_sem=srecv.at[j],
+            device_id=plane_peer(j), device_id_type=MESH)
+        cp.start()
+        ss.append(cp)
+    for cp in ss:
+        cp.wait()
+    m = stat[0, 0]
+    for i in range(1, PLANE):
+        m = jnp.maximum(m, stat[i, 0])
+    s = jnp.zeros_like(m)
+    p = jnp.zeros_like(m)
+    for i in range(PLANE):
+        s = s + stat[i, 1] * jnp.exp(stat[i, 0] - m)
+        p = p + stat[i, 2]
+    own = z * 2 + core
+    lse[...] = p - (m + jnp.log(s))
+    out_ref[own] = lse[...]
+    cs = []
+    for j in range(1, cols):
+        cp = pltpu.make_async_remote_copy(
+            src_ref=lse, dst_ref=out_ref.at[own], send_sem=csend.at[j], recv_sem=crecv.at[j],
+            device_id=col_peer(j), device_id_type=MESH)
+        cp.start()
+        cs.append(cp)
+    for cp in cs:
+        cp.wait()
+
+
+def head_stage(normed, targets, head_z):
+    rows, width = normed.shape
+    zs, vrows, _ = head_z.shape
+    cols = 2 * zs
+    both = jnp.concatenate((targets, targets))
+    lane = jnp.arange(128, dtype=jnp.int32)[None, :]
+    digit = jnp.where(lane == 0, (both % 64)[:, None],
+                      jnp.where(lane == 1, (both // 64 % 64)[:, None],
+                                jnp.where(lane == 2, (both // 4096)[:, None], 0)))
+    digit = digit.astype(jnp.bfloat16)
+    vm = pl.BlockSpec(memory_space=pltpu.VMEM)
+    dma = pltpu.SemaphoreType.DMA
+    n_pad = 16
+    return pl.pallas_call(
+        head_kernel,
+        out_shape=jax.ShapeDtypeStruct((cols, n_pad, 128), jnp.float32),
+        in_specs=[vm, vm, pl.BlockSpec(memory_space=pl.ANY)],
+        out_specs=vm,
+        scratch_shapes=[
+            pltpu.VMEM((PLANE * rows, width), jnp.bfloat16),
+            pltpu.VMEM((PLANE * rows, 128), jnp.bfloat16),
+            pltpu.VMEM((2, zs, vrows, width), jnp.bfloat16),
+            pltpu.VMEM((PLANE, 3, n_pad, 128), jnp.float32),
+            pltpu.VMEM((n_pad, 128), jnp.float32),
+            dma((3,)), dma((PLANE,)), dma((PLANE,)), dma((PLANE,)), dma((PLANE,)),
+            dma((PLANE,)), dma((PLANE,)), dma((cols,)), dma((cols,)),
+        ],
+        compiler_params=pltpu.CompilerParams(
+            collective_id=1, has_side_effects=True, vmem_limit_bytes=60 * 1024 * 1024),
+        name="head_stage",
+    )(normed, digit, head_z)
+
+
+def finish(gathered, tok_count, seq_lengths, owners):
+    cols = gathered.shape[0]
+    zs = cols // 2
+    device_index = lax.axis_index(("grp", "ep"))
+    z = lax.axis_index("grp")
+    ep = lax.axis_index("ep")
+    logprob = gathered[:, : PLANE * 2 * tok_count // 128, :].reshape(zs, 2, PLANE, 2, tok_count)
+    ratio = logprob[:, :, :, 0] - logprob[:, :, :, 1]
+    token_ratio = lax.dynamic_slice(
+        ratio, (z, ep % 2, ep // 2, 0), (1, 1, 1, tok_count)).reshape(tok_count)
+    offsets = jnp.cumsum(seq_lengths) - seq_lengths
+    own = owners == device_index
+    first = jnp.sum(jnp.where(own, offsets, 0))
+    length = jnp.sum(jnp.where(own, seq_lengths, 0))
+    zi = jnp.arange(zs, dtype=jnp.int32)[:, None, None, None]
+    ci = jnp.arange(2, dtype=jnp.int32)[None, :, None, None]
+    si = jnp.arange(PLANE, dtype=jnp.int32)[None, None, :, None]
+    ti = jnp.arange(tok_count, dtype=jnp.int32)[None, None, None, :]
+    pos = ((zi * PLANE + si) * 2 + ci) * tok_count + ti
+    inside = (pos >= first) & (pos < first + length)
+    owned = jnp.sum(jnp.where(inside, ratio, 0.0)) / length.astype(jnp.float32)
+    return token_ratio, owned.reshape(1)
 
 
 def expert_tables(routes, gates, experts, capacity):
@@ -61,7 +220,6 @@
     owners,
 ):
     groups = lax.axis_size("ep")
-    device_index = lax.axis_index(("grp", "ep"))
     local_experts = w_gate.shape[0]
     experts = local_experts * groups
     tok_count = pol_hidden.shape[0]
@@ -101,41 +259,10 @@
 
     pol_normed = mix_back(pol_hidden, pol_mixing, pol_back)
     ref_normed = mix_back(ref_hidden, ref_mixing, ref_back)
-    vocab_rows = vocab_head.shape[0]
-    band = lax.axis_index("grp")
-    pol_col, ref_col, wanted = (
-        lax.all_gather(pol_normed, "grp", axis=0, tiled=True),
-        lax.all_gather(ref_normed, "grp", axis=0, tiled=True),
-        lax.all_gather(targets, "grp", axis=0, tiled=True),
-    )
-    col_count = wanted.shape[0]
-    floor_value = jnp.full((2, col_count), -1e30, jnp.float32)
-    blank = jnp.zeros((2, col_count), jnp.float32)
-    piece = lax.all_gather(vocab_head, "ep", axis=0, tiled=True)
-    count = piece.shape[0]
-    place = jnp.arange(count, dtype=jnp.int32)
-    vocab_ids = band * groups * vocab_rows + place
-    pol_stats = vocab_stats(pol_col, piece, vocab_ids, wanted)
-    ref_stats = vocab_stats(ref_col, piece, vocab_ids, wanted)
-    fresh = tuple(
-        (jnp.stack((pol_part, ref_part)) for pol_part, ref_part in zip(pol_stats, ref_stats))
-    )
-    stats = combine_stats((floor_value, blank, blank), fresh)
-    peak, totals, picked = joined_2(stats, "grp", combine_stats)
-    logprob = picked - (peak + jnp.log(totals))
-    mine = lax.dynamic_slice_in_dim(logprob, band * tok_count, tok_count, axis=1)
-    token_ratio = mine[0] - mine[1]
-    offsets = jnp.cumsum(seq_lengths) - seq_lengths
-    positions = device_index * tok_count + jnp.arange(tok_count, dtype=jnp.int32)
-    inside = (positions[:, None] >= offsets[None, :]) & (
-        positions[:, None] < (offsets + seq_lengths)[None, :]
-    )
-    partial_value = jnp.dot(
-        token_ratio, inside.astype(jnp.float32), precision=lax.Precision.HIGHEST
-    ) / seq_lengths.astype(jnp.float32)
-    sums = lax.psum(partial_value, ("grp", "ep"))
-    owned = jnp.sum(jnp.where(owners == device_index, sums, 0.0)).reshape(1)
-    return (token_ratio, owned)
+    normed = jnp.concatenate((pol_normed, ref_normed), axis=0)
+    head_z = lax.all_gather(vocab_head, "grp", axis=0)
+    gathered = head_stage(normed, targets, head_z)
+    return finish(gathered, tok_count, seq_lengths, owners)
 
 
 def solution(mesh):

time: 391 us -> 231 us (0.59)
  blocking collectives: 222 us -> 0 us
  Pallas kernels: 0 us -> 98.1 us
  matrix products: 38.7 us -> 12.9 us
  other arithmetic: 16.1 us -> 6.46 us
  waiting for transfers between devices: 49.2 us -> 43.2 us
  local copies, waits for them, and re-layouts: 24.4 us -> 28.4 us
    psum x1 -> x0, blocking collectives: 107 us -> none  [local(): sums = lax.psum(partial_value, ('grp', 'ep'))]
    pallas_call x0 -> x1, Pallas kernels: none -> 98.1 us  [head_stage(): pl.pallas_call(head_kernel, out_shape=jax.ShapeDtypeStruct((cols, n_pad,...]
    all_gather x5 -> x0, blocking collectives: 94.7 us -> none  [the longest x3 54 us: joined_2(): pieces = jax.tree.map(lambda part: lax.all_gather(part, axis), value)]
    dot_general x3 -> x0, matrix products: 27.1 us -> none  [the longest x2 26.9 us: vocab_stats(): jnp.einsum('td,vd->tv', row_block, weights, preferred_element_type=jnp.fl...]
    unnamed x1 -> x0, blocking collectives: 20.4 us -> none
    all_to_all x1, waiting for transfers between devices: 21.1 us -> 5.53 us  [local(): lax.all_to_all(outputs[:, :, slots:], 'ep', split_axis=0, concat_axis=0,...]
    all_to_all x1, waiting for transfers between devices: 0.01 us -> 13.5 us  [local(): lax.all_to_all(outputs[:, :, :slots], 'ep', split_axis=0, concat_axis=0,...]
    reduce_sum x2, other arithmetic: 12.1 us -> 2.05 us  [the longest x1 1.35 us: finish(): owned = jnp.sum(jnp.where(inside, ratio, 0.0)) / length.astype(jnp.float32)]
  transfers between devices with their start and end apart: 5 -> 5, of which waited for: 3 -> 4; matrix products, arithmetic and copies ran while one was open for 9% -> 18% of each run, Pallas kernels for 0% -> 0%
where the time goes in v1:
time: 231 us; the launch traced here: 230 us
  Pallas kernels  98.1 us (42%)
  waiting for transfers between devices  43.2 us (19%)
  local copies, waits for them, and re-layouts  28.4 us (12%)
  starting transfers between devices  22.3 us (10%)
  between operations  18.2 us (8%)
  matrix products  12.9 us (6%)
  other arithmetic  6.46 us (3%)
    pallas_call x1, Pallas kernels, head_stage(): pl.pallas_call(head_kernel, out_shape=jax.ShapeDtypeStruct((cols, n_pad,...  98.1 us
    all_to_all x1, waiting for transfers between devices, local(): lax.all_to_all(ref_send, 'ep', split_axis=0, concat_axis=0, tiled=True)  14.2 us
    all_to_all x1, waiting for transfers between devices, local(): lax.all_to_all(outputs[:, :, :slots], 'ep', split_axis=0, concat_axis=0,...  13.5 us
    all_to_all x1, waiting for transfers between devices, local(): lax.all_to_all(pol_send, 'ep', split_axis=0, concat_axis=0, tiled=True)  9.26 us
    all_to_all x1, starting transfers between devices, local(): lax.all_to_all(pol_send, 'ep', split_axis=0, concat_axis=0, tiled=True)  8.72 us
    all_to_all x1, waiting for transfers between devices, local(): lax.all_to_all(outputs[:, :, slots:], 'ep', split_axis=0, concat_axis=0,...  5.53 us
    dot_general x1, matrix products, local(): jnp.einsum('nesf,efd->nesd', inner, w_down, preferred_element_type=jnp.fl...  5.25 us
    unnamed x53, local copies, waits for them, and re-layouts  5.24 us
  transfers between devices with their start and end apart: 5, of which 4 were waited for; matrix products, arithmetic and copies ran while one was open for 18% of the time, Pallas kernels for 0%

profile of v1, /device:TPU:1, one launch (start us, length us, event | category | flops | bytes accessed | tf_op | source)
XLA Modules:
  0.0 229.5 jit_solution(12095754790767650025)
XLA Ops:
  7.2 0.7 all-gather.3.cloned.1.call-update
  7.9 0.8 copy.62
  8.9 0.4 copy-done.11
  9.4 0.6 copy-done.7
  10.4 0.6 copy-done.15
  11.0 0.4 convolution_convert_fusion.1
  11.4 0.3 reshape.398
  11.8 2.0 copy.67
  13.7 8.7 %all-to-all-start = ((bf16[32,2,7,1024]{3,1,2,0:T(2,128)(2,1)}), bf16[32,2,7,1024]{3,1,2,0:T(2,128)(2,1)S(1)}, u32[]{:S(2)}, u32[]{:S(2)}) async-start(bf16[32,2,7,1024]{3,1,2,0:T(2,128)(2,1)} %copy.67), calls=%async_computation | async-start | bytes 1835008 | tf_op jit(solution)/shard_map/all_to_all | solution.py:239
  22.8 0.4 copy-done.13
  23.2 0.6 copy-done.9
  24.1 1.4 convolution_convert_fusion
  25.6 1.4 reshape.399
  27.0 2.0 copy.71
  29.0 9.3 %all-to-all-done = bf16[32,2,7,1024]{3,1,2,0:T(2,128)(2,1)S(1)} async-done(((bf16[32,2,7,1024]{3,1,2,0:T(2,128)(2,1)}), bf16[32,2,7,1024]{3,1,2,0:T(2,128)(2,1)S(1)}, u32[]{:S(2)}, u32[]{:S(2)}) %all-to-all-start) | async-done | bytes 917536 | tf_op jit(solution)/shard_map/all_to_all | solution.py:239
  38.2 4.6 %all-to-all-start.1 = ((bf16[32,2,7,1024]{3,1,2,0:T(2,128)(2,1)}), bf16[32,2,7,1024]{3,1,2,0:T(2,128)(2,1)}, u32[]{:S(2)}, u32[]{:S(2)}) async-start(bf16[32,2,7,1024]{3,1,2,0:T(2,128)(2,1)} %copy.71), calls=%async_computation.1 | async-start | bytes 1835008 | tf_op jit(solution)/shard_map/all_to_all | solution.py:240
  43.0 0.2 select_reduce_fusion
  43.2 1.4 copy_dynamic-update-slice_fusion.1
  44.6 14.2 %all-to-all-done.1 = bf16[32,2,7,1024]{3,1,2,0:T(2,128)(2,1)} async-done(((bf16[32,2,7,1024]{3,1,2,0:T(2,128)(2,1)}), bf16[32,2,7,1024]{3,1,2,0:T(2,128)(2,1)}, u32[]{:S(2)}, u32[]{:S(2)}) %all-to-all-start.1) | async-done | bytes 917536 | tf_op jit(solution)/shard_map/all_to_all | solution.py:240
  58.8 1.5 copy_dynamic-update-slice_fusion
  60.4 0.2 copy-done.4
  60.5 2.2 fusion.5
  62.7 5.3 %convert_bitcast_fusion = bf16[32,2,14,1024]{3,0,2,1:T(8,128)(2,1)} fusion(bf16[2,384,1024]{2,1,0:T(8,128)(2,1)S(1)} %copy-done, bf16[32,2,14,1024]{3,0,2,1:T(8,128)(2,1)S(1)} %copy_dynamic-update-slice_fusion, bf16[2,1024,384]{2,1,0:T(8,128)(2,1)} %param.21, f32[32,2,14,384]{3,0,2,1:T(8,128)} %fusion.5), kind=kOutput, calls=%fused_computation | convolution fusion | flops 1412268032 | bytes 8192000 | tf_op jit(solution)/shard_map/nesf,efd->nesd/dot_general | solution.py:246
  68.0 1.6 fusion.37
  69.6 1.9 copy.78
  71.6 4.1 %all-to-all-start.3 = ((bf16[32,2,7,1024]{3,1,2,0:T(2,128)(2,1)}), bf16[32,2,7,1024]{3,1,2,0:T(2,128)(2,1)S(1)}, u32[]{:S(2)}, u32[]{:S(2)}) async-start(bf16[32,2,7,1024]{3,1,2,0:T(2,128)(2,1)} %copy.78), calls=%async_computation.3 | async-start | bytes 1835008 | tf_op jit(solution)/shard_map/all_to_all | solution.py:250
  75.7 0.8 fusion.23
  76.5 1.6 mul.114
  78.4 0.8 fusion.21
  79.2 1.7 mul.104
  80.9 0.3 reduce-window.9
  81.4 0.7 select_reduce_fusion.3
  84.1 1.9 copy.74
  86.0 5.5 %all-to-all-done.3 = bf16[32,2,7,1024]{3,1,2,0:T(2,128)(2,1)S(1)} async-done(((bf16[32,2,7,1024]{3,1,2,0:T(2,128)(2,1)}), bf16[32,2,7,1024]{3,1,2,0:T(2,128)(2,1)S(1)}, u32[]{:S(2)}, u32[]{:S(2)}) %all-to-all-start.3) | async-done | bytes 917536 | tf_op jit(solution)/shard_map/all_to_all | solution.py:250
  91.6 4.8 %all-to-all-start.2 = ((bf16[32,2,7,1024]{3,1,2,0:T(2,128)(2,1)}), bf16[32,2,7,1024]{3,1,2,0:T(2,128)(2,1)}, u32[]{:S(2)}, u32[]{:S(2)}) async-start(bf16[32,2,7,1024]{3,1,2,0:T(2,128)(2,1)} %copy.74), calls=%async_computation.2 | async-start | bytes 1835008 | tf_op jit(solution)/shard_map/all_to_all | solution.py:249
  96.6 0.7 select_convert_fusion.d_ref
  97.3 0.3 copy.79
  97.5 1.2 reshape.401
  98.8 13.5 %all-to-all-done.2 = bf16[32,2,7,1024]{3,1,2,0:T(2,128)(2,1)} async-done(((bf16[32,2,7,1024]{3,1,2,0:T(2,128)(2,1)}), bf16[32,2,7,1024]{3,1,2,0:T(2,128)(2,1)}, u32[]{:S(2)}, u32[]{:S(2)}) %all-to-all-start.2) | async-done | bytes 917536 | tf_op jit(solution)/shard_map/all_to_all | solution.py:249
  112.3 1.4 copy.75
  113.8 1.3 reshape.400
  115.0 1.8 multiply_reduce_fusion
  116.8 1.8 multiply_reduce_fusion.1
  118.7 0.7 pad_maximum_fusion.x_ref
  119.4 98.1 %head_stage.1 = f32[16,16,128]{2,1,0:T(8,128)} custom-call(bf16[80,1024]{1,0:T(8,128)(2,1)} %pad_maximum_fusion.x_ref, bf16[80,128]{1,0:T(8,128)(2,1)} %select_convert_fusion.d_ref, bf16[8,304,1024]{2,1,0:T(8,128)(2,1)} %bitcast.70), custom_call_target="tpu_custom_call" | custom-call | tf_op jit(solution)/shard_map/head_stage/pallas_call | solution.py:146
  217.5 1.3 reshape.402
  219.0 1.4 select_reduce_fusion.2
  221.0 0.5 dynamic-slice_bitcast_fusion
  (84 shorter events, 2.5 us)
Async XLA Ops:
  7.2 55.6 %copy-start = (bf16[2,384,1024]{2,1,0:T(8,128)(2,1)S(1)}, bf16[2,384,1024]{2,1,0:T(8,128)(2,1)}, u32[]{:S(2)}) copy-start(bf16[2,384,1024]{2,1,0:T(8,128)(2,1)} %param.22) | copy-start | bytes 4718596
  7.2 3.8 %copy-start.6 = (bf16[40,1024]{1,0:T(8,128)(2,1)S(1)}, bf16[40,1024]{1,0:T(8,128)(2,1)}, u32[]{:S(2)}) copy-start(bf16[40,1024]{1,0:T(8,128)(2,1)} %param.14) | copy-start | bytes 245764
  7.2 112.2 %all-gather.3.cloned.1.call-start = ((), (), s32[]{:S(2)}) async-start(), calls=%async_computation.4 | async-start | bytes 5603328 | tf_op jit(solution)/shard_map/all_gather | solution.py:263
  8.7 0.6 copy-start.11
  9.4 0.6 copy-start.7
  10.4 0.6 copy-start.15
  11.7 10.7 %copy-start.19 = (s32[40,8]{0,1:T(8,128)S(1)}, s32[40,8]{0,1:T(8,128)}, u32[]{:S(2)}) copy-start(s32[40,8]{0,1:T(8,128)} %param.17) | copy-start | bytes 3844
  13.7 10.4 %copy-start.5 = (bf16[40,1024]{1,0:T(8,128)(2,1)S(1)}, bf16[40,1024]{1,0:T(8,128)(2,1)}, u32[]{:S(2)}) copy-start(bf16[40,1024]{1,0:T(8,128)(2,1)} %param.15) | copy-start | bytes 245764
  13.7 10.4 %copy-start.16 = (s32[448]{0:T(512)S(1)}, s32[448]{0:T(512)}, u32[]{:S(2)}) copy-start(s32[448]{0:T(512)} %copy-done.15) | copy-start | bytes 5380
  13.7 24.5 %all-to-all-start = ((bf16[32,2,7,1024]{3,1,2,0:T(2,128)(2,1)}), bf16[32,2,7,1024]{3,1,2,0:T(2,128)(2,1)S(1)}, u32[]{:S(2)}, u32[]{:S(2)}) async-start(bf16[32,2,7,1024]{3,1,2,0:T(2,128)(2,1)} %copy.67), calls=%async_computation | async-start | bytes 1835008 | tf_op jit(solution)/shard_map/all_to_all | solution.py:239
  22.6 0.6 copy-start.13
  23.2 0.6 copy-start.9
  29.0 13.9 %copy-start.20 = (f32[40,8]{0,1:T(8,128)S(1)}, f32[40,8]{0,1:T(8,128)}, u32[]{:S(2)}) copy-start(f32[40,8]{0,1:T(8,128)} %param.19) | copy-start | bytes 3844
  29.0 14.0 %copy-start.14 = (s32[40,8]{1,0:T(8,128)S(1)}, s32[40,8]{1,0:T(8,128)}, u32[]{:S(2)}) copy-start(s32[40,8]{1,0:T(8,128)} %copy-done.13) | copy-start | bytes 3844
  38.2 4.9 %copy-start.1 = (bf16[32,2,7,1024]{3,1,2,0:T(2,128)(2,1)}, bf16[32,2,7,1024]{3,1,2,0:T(2,128)(2,1)S(1)}, u32[]{:S(2)}) copy-start(bf16[32,2,7,1024]{3,1,2,0:T(2,128)(2,1)S(1)} %all-to-all-done) | copy-start | bytes 2752516
  38.2 20.6 %all-to-all-start.1 = ((bf16[32,2,7,1024]{3,1,2,0:T(2,128)(2,1)}), bf16[32,2,7,1024]{3,1,2,0:T(2,128)(2,1)}, u32[]{:S(2)}, u32[]{:S(2)}) async-start(bf16[32,2,7,1024]{3,1,2,0:T(2,128)(2,1)} %copy.71), calls=%async_computation.1 | async-start | bytes 1835008 | tf_op jit(solution)/shard_map/all_to_all | solution.py:240
  58.8 1.7 copy-start.4
  69.6 6.1 %copy-start.10 = (s32[40,64]{0,1:T(8,128)S(1)}, s32[40,64]{0,1:T(8,128)}, u32[]{:S(2)}) copy-start(s32[40,64]{0,1:T(8,128)} %copy-done.9) | copy-start | bytes 30724
  71.5 6.6 %copy-start.21 = (f32[40,8]{0,1:T(8,128)S(1)}, f32[40,8]{0,1:T(8,128)}, u32[]{:S(2)}) copy-start(f32[40,8]{0,1:T(8,128)} %param.18) | copy-start | bytes 3844
  71.5 6.7 %copy-start.12 = (s32[40,8]{1,0:T(8,128)S(1)}, s32[40,8]{1,0:T(8,128)}, u32[]{:S(2)}) copy-start(s32[40,8]{1,0:T(8,128)} %copy-done.11) | copy-start | bytes 3844
  71.5 6.9 %copy-start.8 = (s32[40,64]{0,1:T(8,128)S(1)}, s32[40,64]{0,1:T(8,128)}, u32[]{:S(2)}) copy-start(s32[40,64]{0,1:T(8,128)} %copy-done.7) | copy-start | bytes 30724
  71.5 9.3 %copy-start.18 = (s32[256]{0:T(256)S(1)}, s32[256]{0:T(256)}, u32[]{:S(2)}) copy-start(s32[256]{0:T(256)} %param.26) | copy-start | bytes 3076
  71.5 9.9 %copy-start.22 = (s32[256]{0:T(256)S(1)}, s32[256]{0:T(256)}, u32[]{:S(2)}) copy-start(s32[256]{0:T(256)} %param.27) | copy-start | bytes 3076
  71.6 20.0 %all-to-all-start.3 = ((bf16[32,2,7,1024]{3,1,2,0:T(2,128)(2,1)}), bf16[32,2,7,1024]{3,1,2,0:T(2,128)(2,1)S(1)}, u32[]{:S(2)}, u32[]{:S(2)}) async-start(bf16[32,2,7,1024]{3,1,2,0:T(2,128)(2,1)} %copy.78), calls=%async_computation.3 | async-start | bytes 1835008 | tf_op jit(solution)/shard_map/all_to_all | solution.py:250
  84.1 12.3 %copy-start.23 = (s32[40]{0:T(128)S(1)}, s32[40]{0:T(128)}, u32[]{:S(2)}) copy-start(s32[40]{0:T(128)} %param.25) | copy-start | bytes 484
  91.6 20.7 %all-to-all-start.2 = ((bf16[32,2,7,1024]{3,1,2,0:T(2,128)(2,1)}), bf16[32,2,7,1024]{3,1,2,0:T(2,128)(2,1)}, u32[]{:S(2)}, u32[]{:S(2)}) async-start(bf16[32,2,7,1024]{3,1,2,0:T(2,128)(2,1)} %copy.74), calls=%async_computation.2 | async-start | bytes 1835008 | tf_op jit(solution)/shard_map/all_to_all | solution.py:249
  98.8 16.2 %copy-start.2 = (bf16[448,1024]{1,0:T(8,128)(2,1)S(1)}, bf16[448,1024]{1,0:T(8,128)(2,1)}, u32[]{:S(2)}) copy-start(bf16[448,1024]{1,0:T(8,128)(2,1)} %reshape.401) | copy-start | bytes 2752516
  115.0 1.8 copy-start.3
  115.0 3.6 %copy-start.17 = (f32[1024]{0:T(1024)S(1)}, f32[1024]{0:T(1024)}, u32[]{:S(2)}) copy-start(f32[1024]{0:T(1024)} %param.23) | copy-start | bytes 12292
Sparse Core Ops, SparseCore 0:
  9.8 65.9 all-gather.2

commit v2 on v1

v2 whole, which is shorter than its diff:
```python
import jax
import jax.numpy as jnp
from jax import lax
from jax.experimental import pallas as pl
from jax.experimental.pallas import tpu as pltpu
from jax.sharding import PartitionSpec as P

MESH = pl.DeviceIdType.MESH
PLANE = 16
NT = (((1,), (1,)), ((), ()))


def ring_ids(half, d1, d2, piece):
    step = {1: 0, 3: 1, 2: 2 + (piece or 0)}
    inner = step[d1] if d2 == 0 else 4 + d1 * 4 + step[d2]
    return half * 20 + inner


def ring_gather(view, land, near, send_sem, recv_sem, arrived=None):
    sent = []

    def place(half, d1, d2):
        return (d1, d2) if half == 0 else (d2, d1)

    def send(half, d1, d2, piece, second, sign):
        n1, n2 = (d1, (d2 - sign) % 4) if second else ((d1 - sign) % 4, d2)
        k = ring_ids(half, n1, n2, piece)
        axis = (half + second) % 2
        copy = pltpu.make_async_remote_copy(
            src_ref=view(*place(half, d1, d2), half, piece),
            dst_ref=land(*place(half, d1, d2), *place(half, n1, n2), half, piece),
            send_sem=send_sem.at[k], recv_sem=recv_sem.at[k],
            device_id=near(axis, sign), device_id_type=MESH)
        copy.start()
        sent.append(copy)

    def wait(half, d1, d2, piece=None):
        k = ring_ids(half, d1, d2, piece)
        ref = view(*place(half, d1, d2), half, piece)
        pltpu.make_async_remote_copy(
            src_ref=ref, dst_ref=ref, send_sem=send_sem.at[k], recv_sem=recv_sem.at[k],
            device_id=near(0, 1), device_id_type=MESH).wait_recv()

    def full(half, d1, d2):
        if arrived is not None:
            arrived(*place(half, d1, d2), half)

    halves = (0, 1)
    for half in halves:
        send(half, 0, 0, None, 0, 1)
        send(half, 0, 0, None, 0, -1)
    for half in halves:
        send(half, 0, 0, None, 1, 1)
        send(half, 0, 0, None, 1, -1)
        full(half, 0, 0)
    for d1, sign, piece in ((3, 1, 0), (1, -1, 1)):
        for half in halves:
            wait(half, d1, 0)
            send(half, d1, 0, piece, 0, sign)
            send(half, d1, 0, None, 1, 1)
            send(half, d1, 0, None, 1, -1)
            full(half, d1, 0)

    def relay(d1):
        for d2, sign, piece in ((3, 1, 0), (1, -1, 1)):
            for half in halves:
                wait(half, d1, d2)
                send(half, d1, d2, piece, 1, sign)
                full(half, d1, d2)

    relay(0)
    for half in halves:
        wait(half, 2, 0, 0)
        wait(half, 2, 0, 1)
        send(half, 2, 0, None, 1, 1)
        send(half, 2, 0, None, 1, -1)
        full(half, 2, 0)
    for d1 in (3, 1, 2):
        relay(d1)
    for d1 in range(4):
        for half in halves:
            wait(half, d1, 2, 0)
            wait(half, d1, 2, 1)
            full(half, d1, 2)
    return sent


def torus(ep):
    slot = ep // 2
    core = ep % 2
    y = slot // 4
    x = slot % 4

    def at(dx, dy, c):
        return {"ep": (((y + dy) % 4) * 4 + (x + dx) % 4) * 2 + c}

    def near(axis, sign):
        return at(sign, 0, core) if axis == 0 else at(0, sign, core)

    return slot, core, y, x, at, near


def expert_kernel(ph_ref, rh_ref, pr_ref, rr_ref, pg_ref, rg_ref, wg_hbm, wu_hbm, wd_hbm, gain_ref,
                  out_ref, buf, obuf, back, gmat, wg, wu, wd,
                  lsem, wsem, asend, arecv, bsend, brecv, osend, orecv):
    ep = lax.axis_index("ep")
    slot, core, y, x, at, near = torus(ep)
    toks = ph_ref.shape[0]
    rows = 2 * toks
    pad = buf.shape[2] - rows
    width = ph_ref.shape[1]
    f32, bf16 = jnp.float32, jnp.bfloat16
    half_w = width // 2
    quarter = width // 4

    loads = [pltpu.make_async_copy(src, dst, wsem.at[i])
             for i, (src, dst) in enumerate(((wg_hbm, wg), (wu_hbm, wu), (wd_hbm, wd)))]
    for cp in loads:
        cp.start()
    barrier = pltpu.get_barrier_semaphore()
    for r in range(PLANE):
        for c in range(2):
            if r == 0 and c == 1:
                continue
            cc = 1 - core if r == 0 else c
            pl.semaphore_signal(barrier, inc=1, device_id=at(r % 4, r // 4, cc), device_id_type=MESH)
    buf[0, core, pl.ds(0, toks), :] = ph_ref[...]
    buf[0, core, pl.ds(toks, toks), :] = rh_ref[...]

    lane = lax.broadcasted_iota(jnp.int32, (toks, 128), 1)
    token = lax.broadcasted_iota(jnp.int32, (toks, 128), 0).astype(f32)
    lower = (lax.broadcasted_iota(jnp.int32, (toks, toks), 0)
             > lax.broadcasted_iota(jnp.int32, (toks, toks), 1)).astype(bf16)
    ranks, mass, tab = [], [], []
    for model, (routes, gates) in enumerate(((pr_ref, pg_ref), (rr_ref, rg_ref))):
        member = jnp.zeros((toks, 128), f32)
        weight = jnp.zeros((toks, 128), f32)
        for k in range(routes.shape[1]):
            match = routes[:, k:k + 1] == lane
            member = member + jnp.where(match, 1.0, 0.0)
            weight = weight + jnp.where(match, gates[:, k:k + 1], 0.0)
        earlier = jnp.dot(lower, member.astype(bf16), preferred_element_type=f32)
        rank = jnp.where(member > 0.0, earlier, -1.0)
        for s in range(8):
            hit = rank == float(s)
            found = jnp.sum(jnp.where(hit, token + float(model * toks) - 128.0, 0.0), axis=0, keepdims=True)
            tab.append(found + 128.0)
        ranks.append(rank)
        mass.append(weight)
    for r in range(PLANE):
        for c in range(2):
            buf[r, c, pl.ds(rows, pad), pl.ds(half_w, half_w)] = jnp.zeros((pad, half_w), bf16)
    table = jnp.concatenate(tab, axis=0).astype(bf16)
    buf[0, core, pl.ds(rows, pad), pl.ds(0, 128)] = table
    buf[0, core, pl.ds(rows, pad), pl.ds(128, half_w - 128)] = jnp.zeros((pad, half_w - 128), bf16)
    pl.semaphore_wait(barrier, 2 * PLANE - 1)

    def piece_view(dx, dy, half, piece):
        height = rows + pad if half == 0 else rows
        start = half * half_w + (piece or 0) * quarter
        size = half_w if piece is None else quarter
        return buf.at[dy * 4 + dx, core, pl.ds(0, height), pl.ds(start, size)]

    def land(dx, dy, nx, ny, half, piece):
        return piece_view(nx, ny, half, piece)

    across = []

    def arrived(dx, dy, half):
        k = (dy * 4 + dx) * 2 + half
        ref = piece_view(dx, dy, half, None)
        cp = pltpu.make_async_remote_copy(
            src_ref=ref, dst_ref=ref, send_sem=bsend.at[k], recv_sem=brecv.at[k],
            device_id=at(0, 0, 1 - core), device_id_type=MESH)
        cp.start()
        across.append((dx, dy, half, k, cp))

    sent = ring_gather(piece_view, land, near, asend, arecv, arrived)

    lanes = 2 * PLANE * 32
    spread = (lax.broadcasted_iota(jnp.int32, (128, lanes), 1) // 16
              == lax.broadcasted_iota(jnp.int32, (128, lanes), 0)).astype(bf16)
    col = lax.broadcasted_iota(jnp.int32, (toks, lanes), 1)
    for model in range(2):
        hi = mass[model].astype(bf16)
        lo = (mass[model] - hi.astype(f32)).astype(bf16)
        rank = jnp.dot(ranks[model].astype(bf16), spread, preferred_element_type=f32)
        fits = (rank == (col % 8).astype(f32)) & ((col // 8) % 2 == model)
        for part, value in enumerate((hi, lo)):
            wide = jnp.dot(value, spread, preferred_element_type=f32)
            gmat[pl.ds(part * rows + model * toks, toks), :] = jnp.where(fits, wide, 0.0)

    for dx, dy, half, k, cp in across:
        height = rows + pad if half == 0 else rows
        ref = buf.at[dy * 4 + dx, 1 - core, pl.ds(0, height), pl.ds(half * half_w, half_w)]
        pltpu.make_async_remote_copy(
            src_ref=ref, dst_ref=ref, send_sem=bsend.at[k], recv_sem=brecv.at[k],
            device_id=at(0, 0, 1 - core), device_id_type=MESH).wait_recv()
    for cp in loads:
        cp.wait()

    height = rows + pad
    span = PLANE // 2
    count = span * 2 * 16
    deep = span * 2 * height
    sel_lane = lax.broadcasted_iota(jnp.int32, (count, deep), 1)
    tab_lane = lax.broadcasted_iota(jnp.int32, (count, 128), 1)
    block_row = lax.broadcasted_iota(jnp.int32, (count, 1), 0) // 16
    returns = []
    for g in range(2):
        tokens = buf[g * span:(g + 1) * span].reshape(deep, width)
        tabs = buf[g * span:(g + 1) * span, :, rows:rows + pad, 0:128].reshape(count, 128).astype(f32)
        for e in range(2):
            at_e = jnp.sum(jnp.where(tab_lane == ep * 2 + e, tabs, 0.0), axis=1, keepdims=True).astype(jnp.int32)
            index = jnp.where(at_e < 128, at_e + block_row * height, -1)
            pick = (index == sel_lane).astype(bf16)
            taken = jnp.dot(pick, tokens, preferred_element_type=f32).astype(bf16)
            gate = jnp.dot(taken, wg[e], preferred_element_type=f32)
            up = jnp.dot(taken, wu[e], preferred_element_type=f32)
            inner = (gate / (1.0 + jnp.exp(-gate)) * up).astype(bf16)
            out = jnp.dot(inner, wd[e], preferred_element_type=f32).astype(bf16)
            obuf[g * span:(g + 1) * span, :, e * 16:(e + 1) * 16, :] = out.reshape(span, 2, 16, width)
        for r in range(g * span, (g + 1) * span):
            for c in range(2):
                if r == 0:
                    if c == 1:
                        continue
                    cc = 1 - core
                else:
                    cc = c
                cp = pltpu.make_async_remote_copy(
                    src_ref=obuf.at[r, cc], dst_ref=back.at[ep],
                    send_sem=osend.at[r * 2 + c], recv_sem=orecv.at[r * 2 + core],
                    device_id=at(r % 4, r // 4, cc), device_id_type=MESH)
                cp.start()
                returns.append(cp)
    back[ep] = obuf[0, core]
    for r in range(PLANE):
        for c in range(2):
            if r == 0:
                if c == 1:
                    continue
                cc = 1 - core
            else:
                cc = c
            source = at(-(r % 4), -(r // 4), cc)["ep"]
            pltpu.make_async_remote_copy(
                src_ref=back.at[source], dst_ref=back.at[source],
                send_sem=osend.at[r * 2 + c], recv_sem=orecv.at[r * 2 + cc],
                device_id=at(0, 0, 1 - core), device_id_type=MESH).wait_recv()
    parts = jnp.dot(gmat[...].astype(bf16), back[...].reshape(lanes, width), preferred_element_type=f32)
    for model, hidden in enumerate((ph_ref, rh_ref)):
        base = model * toks
        mixed = hidden[...].astype(f32) + (parts[base:base + toks] + parts[rows + base:rows + base + toks])
        scale = lax.rsqrt(jnp.mean(mixed * mixed, axis=1, keepdims=True) + 1e-06)
        out_ref[pl.ds(base, toks), :] = (mixed * scale * gain_ref[...]).astype(bf16)
    for cp in sent:
        cp.wait_send()
    for item in across:
        item[4].wait_send()
    for cp in returns:
        cp.wait_send()


def expert_stage(pol_hidden, ref_hidden, pol_routes, ref_routes, pol_gates, ref_gates, w_gate, w_up, w_down, norm_gain):
    toks, width = pol_hidden.shape
    ff = w_gate.shape[2]
    vm = pl.BlockSpec(memory_space=pltpu.VMEM)
    hbm = pl.BlockSpec(memory_space=pl.ANY)
    dma = pltpu.SemaphoreType.DMA
    bf16 = jnp.bfloat16
    return pl.pallas_call(
        expert_kernel,
        out_shape=jax.ShapeDtypeStruct((2 * toks, width), bf16),
        in_specs=[vm] * 6 + [hbm] * 3 + [vm],
        out_specs=vm,
        scratch_shapes=[
            pltpu.VMEM((PLANE, 2, 2 * toks + 16, width), bf16),
            pltpu.VMEM((PLANE, 2, 32, width), bf16),
            pltpu.VMEM((2 * PLANE, 32, width), bf16),
            pltpu.VMEM((4 * toks, 2 * PLANE * 32), jnp.float32),
            pltpu.VMEM((2, width, ff), bf16),
            pltpu.VMEM((2, width, ff), bf16),
            pltpu.VMEM((2, ff, width), bf16),
            dma((2,)), dma((3,)), dma((40,)), dma((40,)), dma((32,)), dma((32,)), dma((32,)), dma((32,)),
        ],
        compiler_params=pltpu.CompilerParams(
            collective_id=2, has_side_effects=True, vmem_limit_bytes=60 * 1024 * 1024),
        name="expert_stage",
    )(pol_hidden, ref_hidden, pol_routes, ref_routes, pol_gates, ref_gates, w_gate, w_up, w_down,
      norm_gain.reshape(1, width))


def head_kernel(x_ref, hz_ref, out_ref, xbuf, hbuf, stat, lse,
                hsem, xsend, xrecv, ssend, srecv, csend, crecv):
    z = lax.axis_index("grp")
    ep = lax.axis_index("ep")
    slot, core, y, x, at, near = torus(ep)
    zs = lax.axis_size("grp")
    rows = x_ref.shape[0]
    vrows = hz_ref.shape[1]
    cols = 2 * zs

    def plane_peer(j):
        return {"ep": ((slot + j) % PLANE) * 2 + core}

    def col_peer(j):
        other = (z * 2 + core + j) % cols
        return {"grp": other // 2, "ep": slot * 2 + other % 2}

    barrier = pltpu.get_barrier_semaphore()
    for j in range(1, PLANE):
        pl.semaphore_signal(barrier, inc=1, device_id=plane_peer(j), device_id_type=MESH)
    for j in range(1, cols):
        pl.semaphore_signal(barrier, inc=1, device_id=col_peer(j), device_id_type=MESH)
    xbuf[pl.ds(pl.multiple_of(slot * rows, 16), rows), :] = x_ref[...]
    pl.semaphore_wait(barrier, PLANE - 1 + cols - 1)

    width = x_ref.shape[1]

    def view(dx, dy, half, piece):
        where = ((y + dy) % 4) * 4 + (x + dx) % 4
        start, size = ((0, 512), (512, width - 512))[half]
        if piece is not None:
            start, size = ((start, 256), (start + 256, size - 256))[piece]
        return xbuf.at[pl.ds(pl.multiple_of(where * rows, 16), rows), pl.ds(start, size)]

    def land(dx, dy, nx, ny, half, piece):
        return view(dx, dy, half, piece)

    hown = pltpu.make_async_copy(hz_ref, hbuf.at[core], hsem.at[0])
    hown.start()
    hsib = pltpu.make_async_remote_copy(
        src_ref=hz_ref, dst_ref=hbuf.at[core], send_sem=hsem.at[1], recv_sem=hsem.at[2],
        device_id={"ep": slot * 2 + (1 - core)}, device_id_type=MESH)
    hsib.start()
    sent = ring_gather(view, land, near, xsend, xrecv)
    hown.wait()
    hsib.wait()

    stat[slot] = jnp.zeros(stat.shape[1:], jnp.float32)
    lane = lax.broadcasted_iota(jnp.int32, (8, 128), 1)
    weights = jnp.where(lane == 0, 1.0, jnp.where(lane == 1, 64.0, jnp.where(lane == 2, 4096.0, 0.0)))
    weights = weights.astype(jnp.bfloat16)
    tile = 256
    place = lax.broadcasted_iota(jnp.int32, (vrows, tile), 0)

    def tile_body(t, carry):
        rs = pl.ds(pl.multiple_of(t * tile, tile), tile)
        xt = xbuf[rs, pl.ds(0, width - 128)]
        wanted = lax.dot_general(weights, xbuf[rs, pl.ds(width - 128, 128)], NT, preferred_element_type=jnp.float32)
        wanted = wanted[0:1, :].astype(jnp.int32)

        def block(b, state):
            m, s, p = state
            logits = lax.dot_general(hbuf[b // zs, b % zs], xt, NT, preferred_element_type=jnp.float32)
            peak = jnp.maximum(m, jnp.max(logits, axis=0, keepdims=True))
            base = ((b % zs) * (2 * PLANE) + slot * 2 + b // zs) * vrows
            total = s * jnp.exp(m - peak) + jnp.sum(jnp.exp(logits - peak), axis=0, keepdims=True)
            hit = place == (wanted - base)
            got = p + jnp.sum(jnp.where(hit, logits, 0.0), axis=0, keepdims=True)
            return (peak, total, got)

        zero = jnp.zeros((1, tile), jnp.float32)
        m, s, p = lax.fori_loop(0, cols, block, (zero - 1e30, zero, zero), unroll=2)
        for k, v in enumerate((m, s, p)):
            both = jnp.concatenate([v[:, :128], v[:, 128:]], axis=0)
            stat[slot, k, pl.ds(t * 2, 2), :] = both
        return carry

    lax.fori_loop(0, PLANE * rows // tile, tile_body, 0)

    ss = []
    for j in range(1, PLANE):
        cp = pltpu.make_async_remote_copy(
            src_ref=stat.at[slot], dst_ref=stat.at[slot], send_sem=ssend.at[j], recv_sem=srecv.at[j],
            device_id=plane_peer(j), device_id_type=MESH)
        cp.start()
        ss.append(cp)
    for cp in ss:
        cp.wait()
    m = stat[0, 0]
    for i in range(1, PLANE):
        m = jnp.maximum(m, stat[i, 0])
    s = jnp.zeros_like(m)
    p = jnp.zeros_like(m)
    for i in range(PLANE):
        s = s + stat[i, 1] * jnp.exp(stat[i, 0] - m)
        p = p + stat[i, 2]
    own = z * 2 + core
    lse[...] = p - (m + jnp.log(s))
    out_ref[own] = lse[...]
    cs = []
    for j in range(1, cols):
        cp = pltpu.make_async_remote_copy(
            src_ref=lse, dst_ref=out_ref.at[own], send_sem=csend.at[j], recv_sem=crecv.at[j],
            device_id=col_peer(j), device_id_type=MESH)
        cp.start()
        cs.append(cp)
    for cp in cs:
        cp.wait()
    for cp in sent:
        cp.wait_send()


def head_stage(normed, targets, head_z):
    rows, width = normed.shape
    zs, vrows, _ = head_z.shape
    cols = 2 * zs
    both = jnp.concatenate((targets, targets))
    lane = jnp.arange(128, dtype=jnp.int32)[None, :]
    digit = jnp.where(lane == 0, (both % 64)[:, None],
                      jnp.where(lane == 1, (both // 64 % 64)[:, None],
                                jnp.where(lane == 2, (both // 4096)[:, None], 0)))
    digit = digit.astype(jnp.bfloat16)
    vm = pl.BlockSpec(memory_space=pltpu.VMEM)
    dma = pltpu.SemaphoreType.DMA
    n_pad = 16
    return pl.pallas_call(
        head_kernel,
        out_shape=jax.ShapeDtypeStruct((cols, n_pad, 128), jnp.float32),
        in_specs=[vm, pl.BlockSpec(memory_space=pl.ANY)],
        out_specs=vm,
        scratch_shapes=[
            pltpu.VMEM((PLANE * rows, width + 128), jnp.bfloat16),
            pltpu.VMEM((2, zs, vrows, width), jnp.bfloat16),
            pltpu.VMEM((PLANE, 3, n_pad, 128), jnp.float32),
            pltpu.VMEM((n_pad, 128), jnp.float32),
            dma((3,)), dma((40,)), dma((40,)),
            dma((PLANE,)), dma((PLANE,)), dma((cols,)), dma((cols,)),
        ],
        compiler_params=pltpu.CompilerParams(
            collective_id=1, has_side_effects=True, vmem_limit_bytes=60 * 1024 * 1024),
        name="head_stage",
    )(jnp.concatenate((normed, digit), axis=1), head_z)


def finish(gathered, tok_count, seq_lengths, owners):
    cols = gathered.shape[0]
    zs = cols // 2
    device_index = lax.axis_index(("grp", "ep"))
    z = lax.axis_index("grp")
    ep = lax.axis_index("ep")
    logprob = gathered[:, : PLANE * 2 * tok_count // 128, :].reshape(zs, 2, PLANE, 2, tok_count)
    ratio = logprob[:, :, :, 0] - logprob[:, :, :, 1]
    token_ratio = lax.dynamic_slice(
        ratio, (z, ep % 2, ep // 2, 0), (1, 1, 1, tok_count)).reshape(tok_count)
    offsets = jnp.cumsum(seq_lengths) - seq_lengths
    own = owners == device_index
    first = jnp.sum(jnp.where(own, offsets, 0))
    length = jnp.sum(jnp.where(own, seq_lengths, 0))
    zi = jnp.arange(zs, dtype=jnp.int32)[:, None, None, None]
    ci = jnp.arange(2, dtype=jnp.int32)[None, :, None, None]
    si = jnp.arange(PLANE, dtype=jnp.int32)[None, None, :, None]
    ti = jnp.arange(tok_count, dtype=jnp.int32)[None, None, None, :]
    pos = ((zi * PLANE + si) * 2 + ci) * tok_count + ti
    inside = (pos >= first) & (pos < first + length)
    owned = jnp.sum(jnp.where(inside, ratio, 0.0)) / length.astype(jnp.float32)
    return token_ratio, owned.reshape(1)


def local(
    pol_hidden,
    ref_hidden,
    pol_routes,
    ref_routes,
    pol_gates,
    ref_gates,
    w_gate,
    w_up,
    w_down,
    norm_gain,
    vocab_head,
    targets,
    seq_lengths,
    owners,
):
    tok_count = pol_hidden.shape[0]
    normed = expert_stage(pol_hidden, ref_hidden, pol_routes, ref_routes, pol_gates, ref_gates,
                          w_gate, w_up, w_down, norm_gain)
    head_z = lax.all_gather(vocab_head, "grp", axis=0)
    gathered = head_stage(normed, targets, head_z)
    return finish(gathered, tok_count, seq_lengths, owners)


def solution(mesh):
    return jax.shard_map(
        local,
        mesh=mesh,
        in_specs=(
            P(("grp", "ep"), None),
            P(("grp", "ep"), None),
            P(("grp", "ep"), None),
            P(("grp", "ep"), None),
            P(("grp", "ep"), None),
            P(("grp", "ep"), None),
            P("ep", None, None),
            P("ep", None, None),
            P("ep", None, None),
            P(),
            P(("grp", "ep"), None),
            P(("grp", "ep")),
            P(),
            P(),
        ),
        out_specs=(P(("grp", "ep")), P(("grp", "ep"))),
        check_vma=False,
    )
```

time: 231 us -> 172 us (0.74)
  waiting for transfers between devices: 43.2 us -> 0.68 us
  Pallas kernels: 98.1 us -> 139 us
  starting transfers between devices: 22.3 us -> 0.04 us
  local copies, waits for them, and re-layouts: 28.4 us -> 7.51 us
  matrix products: 12.9 us -> 0 us
    pallas_call x0 -> x1, Pallas kernels: none -> 68 us  [expert_stage(): pl.pallas_call(expert_kernel, out_shape=jax.ShapeDtypeStruct((2 * toks, w...]
    all_to_all x4 -> x0, waiting for transfers between devices: 42.5 us -> none  [the longest x1 14.2 us: local(): lax.all_to_all(ref_send, 'ep', split_axis=0, concat_axis=0, tiled=True)]
    pallas_call x1, Pallas kernels: 98.1 us -> 71.3 us  [head_stage(): pl.pallas_call(head_kernel, out_shape=jax.ShapeDtypeStruct((cols, n_pad,...]
    all_to_all x4 -> x0, starting transfers between devices: 22.3 us -> none  [the longest x1 8.72 us: local(): lax.all_to_all(pol_send, 'ep', split_axis=0, concat_axis=0, tiled=True)]
    dot_general x6 -> x0, matrix products: 12.9 us -> none  [the longest x1 5.25 us: local(): jnp.einsum('nesf,efd->nesd', inner, w_down, preferred_element_type=jnp.fl...]
    reshape x6 -> x0, local copies, waits for them, and re-layouts: 8.16 us -> none  [the longest x2 3.4 us: local(): ref_send = ref_send.reshape(groups, local_experts, capacity, width)]
    slice x4 -> x1, local copies, waits for them, and re-layouts: 5.49 us -> 0.07 us  [the longest x2 3.53 us: local(): outputs[:, :, :slots]]
    mul x2 -> x0, local copies, waits for them, and re-layouts: 3.31 us -> none  [expert_tables(): weight[:, :, None] * placed.astype(jnp.float32)]
  transfers between devices with their start and end apart: 5 -> 1, of which waited for: 4 -> 0; matrix products, arithmetic and copies ran while one was open for 18% -> 6% of each run, Pallas kernels for 0% -> 40%
where the time goes in v2:
time: 172 us; the launch traced here: 171 us
  Pallas kernels  139 us (81%)
  between operations  17.9 us (10%)
  local copies, waits for them, and re-layouts  7.51 us (4%)
  other arithmetic  5.81 us (3%)
    pallas_call x1, Pallas kernels, head_stage(): pl.pallas_call(head_kernel, out_shape=jax.ShapeDtypeStruct((cols, n_pad,...  71.3 us
    pallas_call x1, Pallas kernels, expert_stage(): pl.pallas_call(expert_kernel, out_shape=jax.ShapeDtypeStruct((2 * toks, w...  68 us
    unnamed x6, local copies, waits for them, and re-layouts  5.45 us
  transfers between devices with their start and end apart: 1, of which 0 were waited for; matrix products, arithmetic and copies ran while one was open for 6% of the time, Pallas kernels for 40%

profile of v2, /device:TPU:1, one launch (start us, length us, event | category | flops | bytes accessed | tf_op | source)
XLA Modules:
  0.0 171.2 jit_solution(17452020636241700164)
XLA Ops:
  7.2 0.0 all-gather.3.cloned.1.call-start
  7.2 0.7 all-gather.3.cloned.1.call-update
  7.9 1.4 copy.20.pr_ref
  9.3 1.4 copy.21.rr_ref
  10.6 1.4 copy.22.pg_ref
  12.0 1.4 copy.23.rg_ref
  13.4 1.0 reduce-window.9
  14.3 0.1 slice.19
  14.5 0.1 slice_reduce_fusion
  14.6 1.4 select_reduce_fusion.1
  17.9 0.0 copy-start
  17.9 68.0 %expert_stage.1 = bf16[80,1024]{1,0:T(8,128)(2,1)} custom-call(bf16[40,1024]{1,0:T(8,128)(2,1)} %ph_ref.1, bf16[40,1024]{1,0:T(8,128)(2,1)} %rh_ref.1, s32[40,8]{1,0:T(8,128)} %copy.20.pr_ref, s32[40,8]{1,0:T(8,128)} %copy.21.rr_ref, f32[40,8]{1,0:T(8,128)} %copy.22.pg_ref, f32[40,8]{1,0:T(8,128)} %copy.23.rg_ref, bf16[2,1024,384]{2,1,0:T(8,128)(2,1)} %wg_hbm.1, ...), custom_call_target="tpu_custom_call" | custom-call | tf_op jit(solution)/shard_map/expert_stage/pallas_call | solution.py:272
  86.0 0.0 copy-done
  86.0 0.1 and_select_fusion.3
  86.1 0.1 add_multiply_fusion.1
  86.1 0.1 select_convert_fusion
  86.2 1.6 pad_maximum_fusion.x_ref
  87.9 0.0 all-gather.3.cloned.1.call-done
  87.9 71.3 %head_stage.1 = f32[16,16,128]{2,1,0:T(8,128)} custom-call(bf16[80,1152]{1,0:T(8,128)(2,1)} %pad_maximum_fusion.x_ref, bf16[8,304,1024]{2,1,0:T(8,128)(2,1)} %bitcast.14), custom_call_target="tpu_custom_call" | custom-call | tf_op jit(solution)/shard_map/head_stage/pallas_call | solution.py:419
  159.1 1.3 reshape.251
  160.5 0.1 slice_subtract_fusion
  160.7 1.4 select_reduce_fusion
  162.7 0.5 dynamic-slice_bitcast_fusion
  (5 shorter events, 0.1 us)
Async XLA Ops:
  7.2 80.7 %all-gather.3.cloned.1.call-start = ((), (), s32[]{:S(2)}) async-start(), calls=%async_computation | async-start | bytes 5603328 | tf_op jit(solution)/shard_map/all_gather | solution.py:481
  17.9 68.0 %copy-start = (s32[40]{0:T(128)S(1)}, s32[40]{0:T(128)}, u32[]{:S(2)}) copy-start(s32[40]{0:T(128)} %param.25) | copy-start | bytes 484
Sparse Core Ops, SparseCore 0:
  9.8 65.9 all-gather.2

commit v3 on v2

v3 whole, which is shorter than its diff:
```python
import jax
import jax.numpy as jnp
from jax import lax
from jax.experimental import pallas as pl
from jax.experimental.pallas import tpu as pltpu
from jax.sharding import PartitionSpec as P

MESH = pl.DeviceIdType.MESH
PLANE = 16
NT = (((1,), (1,)), ((), ()))


def ring_ids(half, d1, d2, piece):
    step = {1: 0, 3: 1, 2: 2 + (piece or 0)}
    inner = step[d1] if d2 == 0 else 4 + d1 * 4 + step[d2]
    return half * 20 + inner


def ring_gather(view, land, near, send_sem, recv_sem, arrived=None, midway=None):
    sent = []

    def place(half, d1, d2):
        return (d1, d2) if half == 0 else (d2, d1)

    def send(half, d1, d2, piece, second, sign):
        n1, n2 = (d1, (d2 - sign) % 4) if second else ((d1 - sign) % 4, d2)
        k = ring_ids(half, n1, n2, piece)
        axis = (half + second) % 2
        copy = pltpu.make_async_remote_copy(
            src_ref=view(*place(half, d1, d2), half, piece),
            dst_ref=land(*place(half, d1, d2), *place(half, n1, n2), half, piece),
            send_sem=send_sem.at[k], recv_sem=recv_sem.at[k],
            device_id=near(axis, sign), device_id_type=MESH)
        copy.start()
        sent.append(copy)

    def wait(half, d1, d2, piece=None):
        k = ring_ids(half, d1, d2, piece)
        ref = view(*place(half, d1, d2), half, piece)
        pltpu.make_async_remote_copy(
            src_ref=ref, dst_ref=ref, send_sem=send_sem.at[k], recv_sem=recv_sem.at[k],
            device_id=near(0, 1), device_id_type=MESH).wait_recv()

    def full(half, d1, d2):
        if arrived is not None:
            arrived(*place(half, d1, d2), half)

    halves = (0, 1)
    for half in halves:
        send(half, 0, 0, None, 0, 1)
        send(half, 0, 0, None, 0, -1)
    for half in halves:
        send(half, 0, 0, None, 1, 1)
        send(half, 0, 0, None, 1, -1)
        full(half, 0, 0)
    for d1, sign, piece in ((3, 1, 0), (1, -1, 1)):
        for half in halves:
            wait(half, d1, 0)
            send(half, d1, 0, piece, 0, sign)
            send(half, d1, 0, None, 1, 1)
            send(half, d1, 0, None, 1, -1)
            full(half, d1, 0)

    def relay(d1):
        for d2, sign, piece in ((3, 1, 0), (1, -1, 1)):
            for half in halves:
                wait(half, d1, d2)
                send(half, d1, d2, piece, 1, sign)
                full(half, d1, d2)

    relay(0)
    if midway is not None:
        midway()
    for half in halves:
        wait(half, 2, 0, 0)
        wait(half, 2, 0, 1)
        send(half, 2, 0, None, 1, 1)
        send(half, 2, 0, None, 1, -1)
        full(half, 2, 0)
    for d1 in (3, 1, 2):
        relay(d1)
    for d1 in range(4):
        for half in halves:
            wait(half, d1, 2, 0)
            wait(half, d1, 2, 1)
            full(half, d1, 2)
    return sent


def torus(ep):
    slot = ep // 2
    core = ep % 2
    y = slot // 4
    x = slot % 4

    def at(dx, dy, c):
        return {"ep": (((y + dy) % 4) * 4 + (x + dx) % 4) * 2 + c}

    def near(axis, sign):
        return at(sign, 0, core) if axis == 0 else at(0, sign, core)

    return slot, core, y, x, at, near


def kernel(ph_ref, rh_ref, pr_ref, rr_ref, pg_ref, rg_ref, wg_hbm, wu_hbm, wd_hbm, gain_ref,
           head_hbm, tgt_ref, len_ref, own_ref, out_ref,
           buf, obuf, back, gmat, wg, wu, wd, xbuf, hbuf, stat, share, gath,
           wsem, asend, arecv, bsend, brecv, osend, orecv, zsend, zrecv, csend, crecv,
           xsend, xrecv, ssend, srecv, fsend, frecv):
    z = lax.axis_index("grp")
    ep = lax.axis_index("ep")
    zs = lax.axis_size("grp")
    slot, core, y, x, at, near = torus(ep)
    toks = ph_ref.shape[0]
    rows = 2 * toks
    pad = buf.shape[2] - rows
    height = rows + pad
    width = ph_ref.shape[1]
    vrows = head_hbm.shape[0]
    cols = 2 * zs
    f32, bf16 = jnp.float32, jnp.bfloat16
    half_w = width // 2
    quarter = width // 4

    def col_peer(j):
        other = (z * 2 + core + j) % cols
        return {"grp": other // 2, "ep": slot * 2 + other % 2}

    loads = [pltpu.make_async_copy(src, dst, wsem.at[i])
             for i, (src, dst) in enumerate(((wg_hbm, wg), (wu_hbm, wu), (wd_hbm, wd), (head_hbm, hbuf.at[core, z])))]
    for cp in loads:
        cp.start()
    barrier = pltpu.get_barrier_semaphore()
    pairs = [(r, c) for r in range(PLANE) for c in range(2) if (r, c) != (0, 1)]

    def pair(r, c):
        cc = 1 - core if r == 0 else c
        return at(r % 4, r // 4, cc), cc

    for r, c in pairs:
        pl.semaphore_signal(barrier, inc=1, device_id=pair(r, c)[0], device_id_type=MESH)
    for dz in range(1, zs):
        for c in range(2):
            pl.semaphore_signal(barrier, inc=1, device_id={"grp": (z + dz) % zs, "ep": slot * 2 + c},
                                device_id_type=MESH)
    buf[0, core, pl.ds(0, toks), :] = ph_ref[...]
    buf[0, core, pl.ds(toks, toks), :] = rh_ref[...]

    lane = lax.broadcasted_iota(jnp.int32, (toks, 128), 1).astype(f32)
    token = lax.broadcasted_iota(jnp.int32, (toks, 128), 0).astype(f32)
    at_row = lax.broadcasted_iota(jnp.int32, (toks, toks), 0)
    at_col = lax.broadcasted_iota(jnp.int32, (toks, toks), 1)
    lower = (at_row > at_col).astype(bf16)
    same = (at_row == at_col).astype(bf16)
    ranks, mass, tab = [], [], []
    for model, (routes, gates) in enumerate(((pr_ref, pg_ref), (rr_ref, rg_ref))):
        wide = gates[...]
        high = wide.astype(bf16)
        low = (wide - high.astype(f32)).astype(bf16)
        turn = [lax.dot_general(same, v, NT, preferred_element_type=f32)
                for v in (routes[...].astype(f32).astype(bf16), high, low)]
        member = jnp.zeros((toks, 128), f32)
        parts = [member, member]
        for k in range(routes.shape[0]):
            match = turn[0][:, k:k + 1] == lane
            member = member + jnp.where(match, 1.0, 0.0)
            parts = [v + jnp.where(match, t[:, k:k + 1], 0.0) for v, t in zip(parts, turn[1:])]
        earlier = jnp.dot(lower, member.astype(bf16), preferred_element_type=f32)
        rank = jnp.where(member > 0.0, earlier, -1.0)
        for s in range(8):
            hit = rank == float(s)
            found = jnp.sum(jnp.where(hit, token + float(model * toks) - 128.0, 0.0), axis=0, keepdims=True)
            tab.append(found + 128.0)
        ranks.append(rank.astype(bf16))
        mass.append([v.astype(bf16) for v in parts])
    for r in range(PLANE):
        for c in range(2):
            buf[r, c, pl.ds(rows, pad), pl.ds(half_w, half_w)] = jnp.zeros((pad, half_w), bf16)
    table = jnp.concatenate(tab, axis=0).astype(bf16)
    buf[0, core, pl.ds(rows, pad), pl.ds(0, 128)] = table
    buf[0, core, pl.ds(rows, pad), pl.ds(128, half_w - 128)] = jnp.zeros((pad, half_w - 128), bf16)
    pl.semaphore_wait(barrier, len(pairs) + 2 * (zs - 1))

    ring = []

    def z_piece(block, part):
        where = hbuf.at[core, (z + block) % zs]
        if part is None:
            return where
        return where.at[:, pl.ds(part * half_w, half_w)]

    def z_send(block, sign, step):
        part = None if step < 3 else (0 if sign > 0 else 1)
        k = step * 2 + (0 if sign > 0 else 1)
        ref = z_piece(block, part)
        cp = pltpu.make_async_remote_copy(
            src_ref=head_hbm if step == 0 else ref, dst_ref=ref, send_sem=zsend.at[k], recv_sem=zrecv.at[k],
            device_id={"grp": (z + sign) % zs}, device_id_type=MESH)
        cp.start()
        ring.append(cp)

    def z_wait(block, sign, step):
        part = None if step < 3 else (0 if sign > 0 else 1)
        k = step * 2 + (0 if sign > 0 else 1)
        ref = z_piece(block, part)
        pltpu.make_async_remote_copy(
            src_ref=ref, dst_ref=ref, send_sem=zsend.at[k], recv_sem=zrecv.at[k],
            device_id={"grp": (z + sign) % zs}, device_id_type=MESH).wait_recv()

    def cross(block, k, source=None):
        ref = hbuf.at[core, (z + block) % zs]
        cp = pltpu.make_async_remote_copy(
            src_ref=ref if source is None else source, dst_ref=ref, send_sem=csend.at[k], recv_sem=crecv.at[k],
            device_id=at(0, 0, 1 - core), device_id_type=MESH)
        cp.start()
        ring.append(cp)

    def pump(step):
        for sign in (1, -1):
            z_wait(-sign * (step + 1), sign, step)
            z_send(-sign * (step + 1), sign, step + 1)
        for i, sign in enumerate((1, -1)):
            cross(-sign * (step + 1), 1 + step * 2 + i)

    def last_pump():
        for sign in (1, -1):
            z_wait(-sign * 4, sign, 3)
        cross(4, 7)

    z_send(0, 1, 0)
    z_send(0, -1, 0)

    def piece_view(dx, dy, half, piece):
        start = half * half_w + (piece or 0) * quarter
        size = half_w if piece is None else quarter
        return buf.at[dy * 4 + dx, core, pl.ds(0, height if half == 0 else rows), pl.ds(start, size)]

    def land(dx, dy, nx, ny, half, piece):
        return piece_view(nx, ny, half, piece)

    across = []

    def arrived(dx, dy, half):
        k = (dy * 4 + dx) * 2 + half
        ref = piece_view(dx, dy, half, None)
        cp = pltpu.make_async_remote_copy(
            src_ref=ref, dst_ref=ref, send_sem=bsend.at[k], recv_sem=brecv.at[k],
            device_id=at(0, 0, 1 - core), device_id_type=MESH)
        cp.start()
        across.append((dx, dy, half, k, cp))

    sent = ring_gather(piece_view, land, near, asend, arecv, arrived, lambda: pump(0))
    cross(0, 0, head_hbm)

    lanes = 2 * PLANE * 32
    spread = (lax.broadcasted_iota(jnp.int32, (128, lanes), 1) // 16
              == lax.broadcasted_iota(jnp.int32, (128, lanes), 0)).astype(bf16)
    col = lax.broadcasted_iota(jnp.int32, (toks, lanes), 1)
    for model in range(2):
        rank = jnp.dot(ranks[model], spread, preferred_element_type=f32)
        fits = (rank == (col % 8).astype(f32)) & ((col // 8) % 2 == model)
        for part, value in enumerate(mass[model]):
            wide = jnp.dot(value, spread, preferred_element_type=f32)
            gmat[pl.ds(part * rows + model * toks, toks), :] = jnp.where(fits, wide, 0.0)

    for dx, dy, half, k, cp in across:
        ref = buf.at[dy * 4 + dx, 1 - core, pl.ds(0, height if half == 0 else rows), pl.ds(half * half_w, half_w)]
        pltpu.make_async_remote_copy(
            src_ref=ref, dst_ref=ref, send_sem=bsend.at[k], recv_sem=brecv.at[k],
            device_id=at(0, 0, 1 - core), device_id_type=MESH).wait_recv()
    for cp in loads:
        cp.wait()

    span = PLANE // 2
    count = span * 2 * 16
    deep = span * 2 * height
    sel_lane = lax.broadcasted_iota(jnp.int32, (count, deep), 1)
    tab_lane = lax.broadcasted_iota(jnp.int32, (count, 128), 1)
    block_row = lax.broadcasted_iota(jnp.int32, (count, 1), 0) // 16
    returns = []
    for g in range(2):
        tokens = buf[g * span:(g + 1) * span].reshape(deep, width)
        tabs = buf[g * span:(g + 1) * span, :, rows:rows + pad, 0:128].reshape(count, 128).astype(f32)
        for e in range(2):
            at_e = jnp.sum(jnp.where(tab_lane == ep * 2 + e, tabs, 0.0), axis=1, keepdims=True).astype(jnp.int32)
            index = jnp.where(at_e < 128, at_e + block_row * height, -1)
            pick = (index == sel_lane).astype(bf16)
            taken = jnp.dot(pick, tokens, preferred_element_type=f32).astype(bf16)
            gate = jnp.dot(taken, wg[e], preferred_element_type=f32)
            up = jnp.dot(taken, wu[e], preferred_element_type=f32)
            inner = (gate / (1.0 + jnp.exp(-gate)) * up).astype(bf16)
            out = jnp.dot(inner, wd[e], preferred_element_type=f32).astype(bf16)
            obuf[g * span:(g + 1) * span, :, e * 16:(e + 1) * 16, :] = out.reshape(span, 2, 16, width)
        for r, c in pairs:
            if r // span != g:
                continue
            dev, cc = pair(r, c)
            cp = pltpu.make_async_remote_copy(
                src_ref=obuf.at[r, cc], dst_ref=back.at[ep],
                send_sem=osend.at[r * 2 + c], recv_sem=orecv.at[r * 2 + core],
                device_id=dev, device_id_type=MESH)
            cp.start()
            returns.append(cp)
        if g == 0:
            pump(1)
    back[ep] = obuf[0, core]
    pump(2)
    for r, c in pairs:
        cc = 1 - core if r == 0 else c
        source = at(-(r % 4), -(r // 4), cc)["ep"]
        pltpu.make_async_remote_copy(
            src_ref=back.at[source], dst_ref=back.at[source],
            send_sem=osend.at[r * 2 + c], recv_sem=orecv.at[r * 2 + cc],
            device_id=at(0, 0, 1 - core), device_id_type=MESH).wait_recv()
    mixing = jnp.dot(gmat[...].astype(bf16), back[...].reshape(lanes, width), preferred_element_type=f32)
    here = pl.multiple_of(slot * rows, 16)
    normed = []
    for model, hidden in enumerate((ph_ref, rh_ref)):
        base = model * toks
        mixed = hidden[...].astype(f32) + (mixing[base:base + toks] + mixing[rows + base:rows + base + toks])
        scale = lax.rsqrt(jnp.mean(mixed * mixed, axis=1, keepdims=True) + 1e-06)
        normed.append(mixed * scale * gain_ref[...])
    xbuf[pl.ds(here, rows), pl.ds(0, width)] = jnp.concatenate(normed, axis=0).astype(bf16)
    tgt = jnp.broadcast_to(tgt_ref[...], (128, toks))
    kind = lax.broadcasted_iota(jnp.int32, (128, toks), 0)
    digit = jnp.where(kind == 0, tgt & 63, jnp.where(kind == 1, (tgt >> 6) & 63, jnp.where(kind == 2, tgt >> 12, 0)))
    digit = lax.dot_general(same, digit.astype(f32).astype(bf16), NT, preferred_element_type=f32)
    xbuf[pl.ds(here, rows), pl.ds(width, 128)] = jnp.concatenate((digit, digit), axis=0).astype(bf16)

    def view(dx, dy, half, piece):
        where = ((y + dy) % 4) * 4 + (x + dx) % 4
        start, size = ((0, half_w), (half_w, half_w + 128))[half]
        if piece is not None:
            start, size = ((start, quarter), (start + quarter, size - quarter))[piece]
        return xbuf.at[pl.ds(pl.multiple_of(where * rows, 16), rows), pl.ds(start, size)]

    sent += ring_gather(view, lambda dx, dy, nx, ny, half, piece: view(dx, dy, half, piece), near, xsend, xrecv,
                        None, last_pump)
    for k in range(8):
        block = (0, -1, 1, -2, 2, -3, 3, 4)[k]
        ref = hbuf.at[1 - core, (z + block) % zs]
        pltpu.make_async_remote_copy(
            src_ref=ref, dst_ref=ref, send_sem=csend.at[k], recv_sem=crecv.at[k],
            device_id=at(0, 0, 1 - core), device_id_type=MESH).wait_recv()

    stat[slot] = jnp.zeros(stat.shape[1:], f32)
    out_ref[...] = jnp.zeros(out_ref.shape, f32)
    power = lax.broadcasted_iota(jnp.int32, (8, 128), 1)
    power = jnp.where(power == 0, 1.0, jnp.where(power == 1, 64.0, jnp.where(power == 2, 4096.0, 0.0)))
    power = power.astype(bf16)
    tile = 256
    place = lax.broadcasted_iota(jnp.int32, (vrows, tile), 0)

    def tile_body(t, carry):
        rs = pl.ds(pl.multiple_of(t * tile, tile), tile)
        xt = xbuf[rs, pl.ds(0, width)]
        wanted = lax.dot_general(power, xbuf[rs, pl.ds(width, 128)], NT, preferred_element_type=f32)
        wanted = wanted[0:1, :].astype(jnp.int32)

        def block(b, state):
            m, s, p = state
            logits = lax.dot_general(hbuf[b // zs, b % zs], xt, NT, preferred_element_type=f32)
            peak = jnp.maximum(m, jnp.max(logits, axis=0, keepdims=True))
            first = ((b % zs) * (2 * PLANE) + slot * 2 + b // zs) * vrows
            total = s * jnp.exp(m - peak) + jnp.sum(jnp.exp(logits - peak), axis=0, keepdims=True)
            hit = place == (wanted - first)
            got = p + jnp.sum(jnp.where(hit, logits, 0.0), axis=0, keepdims=True)
            return (peak, total, got)

        zero = jnp.zeros((1, tile), f32)
        m, s, p = lax.fori_loop(0, cols, block, (zero - 1e30, zero, zero), unroll=2)
        for k, v in enumerate((m, s, p)):
            stat[slot, k, pl.ds(t * 2, 2), :] = jnp.concatenate([v[:, :128], v[:, 128:]], axis=0)
        return carry

    lax.fori_loop(0, PLANE * rows // tile, tile_body, 0)

    swap = []
    for r in range(1, PLANE):
        cp = pltpu.make_async_remote_copy(
            src_ref=stat.at[slot], dst_ref=stat.at[slot], send_sem=ssend.at[r], recv_sem=srecv.at[r],
            device_id=at(r % 4, r // 4, core), device_id_type=MESH)
        cp.start()
        swap.append(cp)
    index = z * (2 * PLANE) + ep
    number = (lax.broadcasted_iota(jnp.int32, own_ref.shape, 0) * own_ref.shape[1]
              + lax.broadcasted_iota(jnp.int32, own_ref.shape, 1))
    mine = own_ref[...] == index
    lens = len_ref[...].astype(f32)

    def total(v):
        return jnp.sum(jnp.sum(v, axis=0, keepdims=True), axis=1, keepdims=True)

    ordinal = total(jnp.where(mine, number, 0).astype(f32))
    length = total(jnp.where(mine, lens, 0.0))
    first = total(jnp.where(number.astype(f32) < ordinal, lens, 0.0))
    for r in range(1, PLANE):
        source = at(-(r % 4), -(r // 4), core)["ep"] // 2
        pltpu.make_async_remote_copy(
            src_ref=stat.at[source], dst_ref=stat.at[source], send_sem=ssend.at[r], recv_sem=srecv.at[r],
            device_id=at(0, 0, 1 - core), device_id_type=MESH).wait_recv()
    m = stat[0, 0]
    for i in range(1, PLANE):
        m = jnp.maximum(m, stat[i, 0])
    s = jnp.zeros_like(m)
    p = jnp.zeros_like(m)
    for i in range(PLANE):
        s = s + stat[i, 1] * jnp.exp(stat[i, 0] - m)
        p = p + stat[i, 2]
    logprob = p - (m + jnp.log(s))
    lines = PLANE * rows // 128
    flat = jnp.concatenate([logprob[i:i + 1, :] for i in range(lines)], axis=1)
    ratio = flat - pltpu.roll(flat, lines * 128 - toks, 1)
    share[...] = jnp.concatenate([ratio[:, i * 128:(i + 1) * 128] for i in range(lines)]
                                 + [jnp.zeros((16 - lines, 128), f32)], axis=0)
    gath[z * 2 + core] = share[...]
    for j in range(1, cols):
        cp = pltpu.make_async_remote_copy(
            src_ref=share, dst_ref=gath.at[z * 2 + core], send_sem=fsend.at[j], recv_sem=frecv.at[j],
            device_id=col_peer(j), device_id_type=MESH)
        cp.start()
        swap.append(cp)
    out_ref[0:1, :] = pltpu.roll(ratio, (lines * 128 - slot * rows) % (lines * 128), 1)[:, 0:128]
    for j in range(1, cols):
        source = (z * 2 + core + cols - j) % cols
        pltpu.make_async_remote_copy(
            src_ref=share, dst_ref=gath.at[source], send_sem=fsend.at[j], recv_sem=frecv.at[j],
            device_id=col_peer(j), device_id_type=MESH).wait_recv()
    shape = (16, 128)
    spot = lax.broadcasted_iota(jnp.int32, shape, 0) * 128 + lax.broadcasted_iota(jnp.int32, shape, 1)
    from_slot = ((spot.astype(f32) + 0.5) * (1.0 / rows)).astype(jnp.int32)
    rest = spot - from_slot * rows
    live = (rest < toks) & (spot < lines * 128)
    owned = jnp.zeros(shape, f32)
    for i in range(cols):
        position = (((i // 2) * PLANE + from_slot) * 2 + i % 2) * toks + rest
        position = position.astype(f32)
        inside = live & (position >= first) & (position < first + length)
        owned = owned + jnp.where(inside, gath[i], 0.0)
    out_ref[1:2, :] = jnp.broadcast_to(total(owned) / length, (1, 128))
    for cp in sent + returns + ring + swap:
        cp.wait_send()
    for item in across:
        item[4].wait_send()


def local(pol_hidden, ref_hidden, pol_routes, ref_routes, pol_gates, ref_gates, w_gate, w_up, w_down, norm_gain,
          vocab_head, targets, seq_lengths, owners):
    toks, width = pol_hidden.shape
    ff = w_gate.shape[2]
    zs = lax.axis_size("grp")
    vrows = vocab_head.shape[0]
    cols = 2 * zs
    bf16, f32 = jnp.bfloat16, jnp.float32
    vm = pl.BlockSpec(memory_space=pltpu.VMEM)
    hbm = pl.BlockSpec(memory_space=pl.ANY)
    dma = pltpu.SemaphoreType.DMA
    out = pl.pallas_call(
        kernel,
        out_shape=jax.ShapeDtypeStruct((8, 128), f32),
        in_specs=[vm] * 6 + [hbm] * 3 + [vm, hbm] + [vm] * 3,
        out_specs=vm,
        scratch_shapes=[
            pltpu.VMEM((PLANE, 2, 2 * toks + 16, width), bf16),
            pltpu.VMEM((PLANE, 2, 32, width), bf16),
            pltpu.VMEM((2 * PLANE, 32, width), bf16),
            pltpu.VMEM((4 * toks, 2 * PLANE * 32), f32),
            pltpu.VMEM((2, width, ff), bf16),
            pltpu.VMEM((2, width, ff), bf16),
            pltpu.VMEM((2, ff, width), bf16),
            pltpu.VMEM((PLANE * 2 * toks, width + 128), bf16),
            pltpu.VMEM((2, zs, vrows, width), bf16),
            pltpu.VMEM((PLANE, 3, 16, 128), f32),
            pltpu.VMEM((16, 128), f32),
            pltpu.VMEM((cols, 16, 128), f32),
            dma((4,)), dma((40,)), dma((40,)), dma((32,)), dma((32,)), dma((32,)), dma((32,)),
            dma((8,)), dma((8,)), dma((8,)), dma((8,)), dma((40,)), dma((40,)),
            dma((PLANE,)), dma((PLANE,)), dma((cols,)), dma((cols,)),
        ],
        compiler_params=pltpu.CompilerParams(
            collective_id=1, has_side_effects=True, vmem_limit_bytes=62 * 1024 * 1024),
        name="whole",
    )(pol_hidden, ref_hidden, pol_routes.T, ref_routes.T, pol_gates.T, ref_gates.T, w_gate, w_up, w_down,
      norm_gain.reshape(1, width), vocab_head, targets.reshape(1, toks),
      seq_lengths.reshape(-1, 128), owners.reshape(-1, 128))
    return out[0, :toks], out[1, :1]


def solution(mesh):
    return jax.shard_map(
        local,
        mesh=mesh,
        in_specs=(
            P(("grp", "ep"), None),
            P(("grp", "ep"), None),
            P(("grp", "ep"), None),
            P(("grp", "ep"), None),
            P(("grp", "ep"), None),
            P(("grp", "ep"), None),
            P("ep", None, None),
            P("ep", None, None),
            P("ep", None, None),
            P(),
            P(("grp", "ep"), None),
            P(("grp", "ep")),
            P(),
            P(),
        ),
        out_specs=(P(("grp", "ep")), P(("grp", "ep"))),
        check_vma=False,
    )
```

time: 172 us -> 145 us (0.84)
  between operations: 17.9 us -> 0.64 us
  other arithmetic: 5.81 us -> 0 us
  local copies, waits for them, and re-layouts: 7.51 us -> 2.39 us
  Pallas kernels: 139 us -> 142 us
    unnamed x6 -> x0, local copies, waits for them, and re-layouts: 5.45 us -> none
    reduce_sum x2 -> x0, other arithmetic: 2.75 us -> none  [the longest x1 1.4 us: finish(): length = jnp.sum(jnp.where(own, seq_lengths, 0))]
    pallas_call x2 -> x1, Pallas kernels: 139 us -> 142 us  [local(): pl.pallas_call(kernel, out_shape=jax.ShapeDtypeStruct((8, 128), f32), in_...]
    reshape x2 -> x0, local copies, waits for them, and re-layouts: 1.87 us -> none  [the longest x1 1.35 us: finish(): gathered[:, :PLANE * 2 * tok_count // 128, :]]
  transfers between devices with their start and end apart: 1 -> 0, of which waited for: 0 -> 0; matrix products, arithmetic and copies ran while one was open for 6% -> 0% of each run, Pallas kernels for 40% -> 0%
where the time goes in v3:
time: 145 us
  Pallas kernels  142 us (98%)
  local copies, waits for them, and re-layouts  2.39 us (2%)
    pallas_call x1, Pallas kernels, local(): pl.pallas_call(kernel, out_shape=jax.ShapeDtypeStruct((8, 128), f32), in_...  142 us

profile of v3, /device:TPU:1, one launch (start us, length us, event | category | flops | bytes accessed | tf_op | source)
XLA Modules:
  0.0 144.9 jit_solution(8927589867896259664)
XLA Ops:
  0.6 141.9 %whole.1 = f32[8,128]{1,0:T(8,128)} custom-call(bf16[40,1024]{1,0:T(8,128)(2,1)} %ph_ref.1, bf16[40,1024]{1,0:T(8,128)(2,1)} %rh_ref.1, s32[8,40]{1,0:T(8,128)} %bitcast.11, s32[8,40]{1,0:T(8,128)} %bitcast.12, f32[8,40]{1,0:T(8,128)} %bitcast.13, f32[8,40]{1,0:T(8,128)} %bitcast.14, bf16[2,1024,384]{2,1,0:T(8,128)(2,1)} %wg_hbm.1, ...), custom_call_target="tpu_custom_call" | custom-call | tf_op jit(solution)/shard_map/whole/pallas_call | solution.py:458
  142.5 1.2 slice.7
  143.7 1.2 slice_bitcast_fusion
